TPU v7x, 256 devices: a whole 4x4x8 slice. The times are simulated.
256 devices in a mesh: dp: 32 (over x, z), block: 8 (over y, core).
Axes of the slice: x: 4, y: 4, z: 8, core: 2. Of those that a mesh axis runs over, the one named last changes fastest.
Arguments:
- tokens: bfloat16 [32, 256, 4096], P('dp', 'block'), may hold values from -6 to 6
- cotangent: bfloat16 [32, 256, 4096], P('dp', 'block'), may hold values from -6 to 6
- w_up: bfloat16 [8, 4096, 512], P('block'), may hold values from -0.09375 to 0.09375
- w_down: bfloat16 [8, 512, 4096], P('block'), may hold values from -0.25 to 0.25
- active: int32 [32, 8], replicated, may hold values from 0 to 1, as said below
- width: int32 [32], replicated, may hold values from 8 to 16
- counts: int32 [8], replicated, may hold values from 32 to 127
Outputs:
- mixed: bfloat16 [32, 256, 4096], P('dp', 'block')
- input_grad: bfloat16 [32, 256, 4096], P('dp', 'block')
- up_grad: float32 [8, 4096, 512], P('block', 'dp')
- down_grad: float32 [8, 512, 4096], P('block', None, 'dp')
Inputs may be any that keep to these rules, and one draw needn't show every extreme that they name: `active`: 0 or 1; blocks differ in how many micro-batches use them. micro-batch i uses the first 256 * width[i] features.
All inputs are finite; a program needn't handle non-finite values.
Results may differ from a plain program's by a relative error of at most 0.019.
Values may be sent and summed in bfloat16 or wider, within the bound.
No kernel may reach another device: no remote copies, remote signals or barrier semaphores. Data moves between devices by JAX's collectives and lax.ppermute only.
A program may use at most 128 MiB of HBM per device.

v0:
```python
import math

import jax
import jax.numpy as jnp
from jax import lax
from jax.sharding import PartitionSpec as P

GELU_C = math.sqrt(2.0 / math.pi)


def gelu_parts(pre_vals):
    tanh_val = jnp.tanh(GELU_C * (pre_vals + 0.044715 * pre_vals * pre_vals * pre_vals))
    gelu_value = 0.5 * pre_vals * (1.0 + tanh_val)
    gelu_slope = 0.5 * (1.0 + tanh_val) + 0.5 * pre_vals * (1.0 - tanh_val * tanh_val) * GELU_C * (
        1.0 + 3.0 * 0.044715 * pre_vals * pre_vals
    )
    return (gelu_value, gelu_slope)


def local(tokens, cotangent, w_up, w_down, active, width, counts):
    micro_index = lax.axis_index("dp")
    owner_index = lax.axis_index("block")
    local_count = w_up.shape[0]
    feats = tokens.shape[2]
    start_block = owner_index * local_count
    act_row = lax.dynamic_slice(active, (micro_index, start_block), (1, local_count))[0]
    gate_row = act_row.astype(jnp.float32)
    counts_here = lax.dynamic_slice(counts, (start_block,), (local_count,)).astype(jnp.float32)
    scale_row = gate_row / counts_here
    width_step = lax.dynamic_slice(width, (micro_index,), (1,))[0]
    width_limit = feats // 16 * width_step
    feat_mask = (lax.iota(jnp.int32, feats) < width_limit).astype(jnp.bfloat16)
    gathered = (
        lax.all_gather(tokens, "block", axis=1, tiled=True),
        lax.all_gather(cotangent, "block", axis=1, tiled=True),
    )
    whole_x = gathered[0][0]
    whole_dy = gathered[1][0]
    masked_x = whole_x * feat_mask
    masked_dy = whole_dy * feat_mask
    pre_act = jnp.einsum("rd,bdu->bru", masked_x, w_up, preferred_element_type=jnp.float32)
    gelu_value, gelu_slope = gelu_parts(pre_act)
    hidden = gelu_value.astype(jnp.bfloat16)
    products = jnp.einsum("bru,bud->brd", hidden, w_down, preferred_element_type=jnp.float32)
    mixed_sum = lax.psum_scatter(
        jnp.sum(products * gate_row[:, None, None], axis=0).astype(jnp.bfloat16),
        "block",
        scatter_dimension=0,
        tiled=True,
    ).astype(jnp.float32)
    down_term = scale_row[:, None, None] * jnp.einsum(
        "bru,rd->bud", hidden, masked_dy, preferred_element_type=jnp.float32
    )
    back_proj = jnp.einsum("rd,bud->bru", masked_dy, w_down, preferred_element_type=jnp.float32)
    grad_hidden = (back_proj * gelu_slope).astype(jnp.bfloat16)
    up_term = scale_row[:, None, None] * jnp.einsum(
        "rd,bru->bdu", masked_x, grad_hidden, preferred_element_type=jnp.float32
    )
    up_grad, down_grad = (
        lax.psum_scatter(
            up_term.astype(jnp.bfloat16), "dp", scatter_dimension=1, tiled=True
        ).astype(jnp.float32),
        lax.psum_scatter(
            down_term.astype(jnp.bfloat16), "dp", scatter_dimension=2, tiled=True
        ).astype(jnp.float32),
    )
    products = jnp.einsum("bru,bdu->brd", grad_hidden, w_up, preferred_element_type=jnp.float32)
    input_sum = lax.psum_scatter(
        jnp.sum(products * gate_row[:, None, None], axis=0).astype(jnp.bfloat16),
        "block",
        scatter_dimension=0,
        tiled=True,
    ).astype(jnp.float32)
    mask_float = feat_mask.astype(jnp.float32)
    mixed = (tokens[0].astype(jnp.float32) + mask_float * mixed_sum).astype(jnp.bfloat16)[None]
    input_grad = (cotangent[0].astype(jnp.float32) + mask_float * input_sum).astype(jnp.bfloat16)[
        None
    ]
    return (mixed, input_grad, up_grad, down_grad)


def solution(mesh):
    in_specs = (
        P("dp", "block", None),
        P("dp", "block", None),
        P("block", None, None),
        P("block", None, None),
        P(),
        P(),
        P(),
    )
    out_specs = (
        P("dp", "block", None),
        P("dp", "block", None),
        P("block", "dp", None),
        P("block", None, "dp"),
    )
    return jax.shard_map(local, mesh=mesh, in_specs=in_specs, out_specs=out_specs, check_vma=False)
```

profile of v0, /device:TPU:6, one launch (start us, length us, event | category | flops | bytes accessed | tf_op | source)
XLA Modules:
  0.0 607.3 jit_solution(4567592196904731173)
XLA Ops:
  7.9 0.7 all-gather.5.cloned.1.call-update
  8.7 1.2 dynamic_slice.9
  9.9 1.3 dynamic_slice.10
  12.5 28.0 %all-gather.3.cloned.1.call-done = bf16[1,256,4096]{2,1,0:T(8,128)(2,1)} async-done(((bf16[1,32,4096]{2,1,0:T(8,128)(2,1)}), bf16[1,256,4096]{2,1,0:T(8,128)(2,1)}) %all-gather.3.cloned.1.call-update) | async-done | bytes 2097168 | tf_op jit(solution)/shard_map/all_gather | solution.py:34
  40.5 4.1 fusion.18
  44.6 25.9 %all-gather.5.cloned.1.call-done = bf16[1,256,4096]{2,1,0:T(8,128)(2,1)} async-done(((bf16[1,32,4096]{2,1,0:T(8,128)(2,1)}), bf16[1,256,4096]{2,1,0:T(8,128)(2,1)}) %all-gather.5.cloned.1.call-update) | async-done | bytes 2097168 | tf_op jit(solution)/shard_map/all_gather | solution.py:35
  70.5 4.4 fusion.38
  74.9 2.7 fusion.3
  77.7 5.0 fusion.2
  84.1 3.3 fusion
  87.3 19.0 %copy.13 = bf16[1,4096,512]{2,0,1:T(2,128)(2,1)} copy(bf16[1,4096,512]{1,2,0:T(8,128)(2,1)} %fusion) | data formatting | bytes 8388608
  106.3 6.7 %copy.22 = bf16[4096,1,512]{2,0,1:T(8,128)(2,1)} copy(bf16[4096,1,512]{2,1,0:T(2,128)(2,1)} %bitcast.100) | data formatting | bytes 8388608
  113.1 1.6 copy-done.4
  114.6 3.3 fusion.1
  118.0 19.0 %copy.15 = bf16[1,512,4096]{1,0,2:T(2,128)(2,1)} copy(bf16[1,512,4096]{2,1,0:T(8,128)(2,1)} %fusion.1) | data formatting | bytes 8388608
  136.9 6.7 %copy.21 = bf16[4096,1,512]{2,0,1:T(8,128)(2,1)} copy(bf16[4096,1,512]{2,1,0:T(2,128)(2,1)} %bitcast.101) | data formatting | bytes 8388608
  143.7 8.0 %reduce-scatter.9.cloned.1.call-done = bf16[32,4096]{1,0:T(8,128)(2,1)} async-done(((bf16[256,4096]{1,0:T(8,128)(2,1)}), bf16[32,4096]{1,0:T(8,128)(2,1)}) %reduce-scatter.9.cloned.1.call-update) | async-done | bytes 262160 | tf_op jit(solution)/shard_map/reduce_scatter | solution.py:45
  151.7 2.0 fusion.55
  153.7 221.1 %reduce-scatter.13.cloned.1.call-done = bf16[128,512]{1,0:T(8,128)(2,1)} async-done(((bf16[4096,512]{1,0:T(8,128)(2,1)}), bf16[128,512]{1,0:T(8,128)(2,1)}) %reduce-scatter.13.cloned.1.call-update) | async-done | bytes 131088
  374.8 1.0 reshape_bitcast_fusion.1
  376.0 0.8 copy.12
  376.8 221.7 %reduce-scatter.15.cloned.1.call-done = bf16[128,512]{1,0:T(8,128)(2,1)} async-done(((bf16[4096,512]{1,0:T(8,128)(2,1)}), bf16[128,512]{1,0:T(8,128)(2,1)}) %reduce-scatter.15.cloned.1.call-update) | async-done | bytes 131088
  598.5 1.0 reshape_bitcast_fusion
  599.7 0.7 convert_element_type.106
  (28 shorter events, 2.0 us)
Async XLA Ops:
  7.2 33.4 %all-gather.3.cloned.1.call-start = ((), (), s32[]{:S(2)}) async-start(), calls=%async_computation.4 | async-start | bytes 2359296 | tf_op jit(solution)/shard_map/all_gather | solution.py:34
  7.9 62.6 %all-gather.5.cloned.1.call-start = ((), (), s32[]{:S(2)}) async-start(), calls=%async_computation.6 | async-start | bytes 2359296 | tf_op jit(solution)/shard_map/all_gather | solution.py:35
  8.6 135.0 %reduce-scatter.11.cloned.1.call-start = ((), (), s32[]{:S(2)}) async-start(), calls=%async_computation.7 | async-start | bytes 2359296 | tf_op jit(solution)/shard_map/reduce_scatter | solution.py:68
  70.5 4.4 copy-start.3
  77.7 5.1 copy-start.5
  77.7 6.4 %copy-start = (bf16[1,256,4096]{2,1,0:T(8,128)(2,1)S(1)}, bf16[1,256,4096]{2,1,0:T(8,128)(2,1)}, u32[]{:S(2)}) copy-start(bf16[1,256,4096]{2,1,0:T(8,128)(2,1)} %all-gather.3.cloned.1.call-done) | copy-start | bytes 6291460
  77.7 74.0 %reduce-scatter.9.cloned.1.call-start = ((), (), s32[]{:S(2)}) async-start(), calls=%async_computation.5 | async-start | bytes 2359296 | tf_op jit(solution)/shard_map/reduce_scatter | solution.py:45
  82.7 292.1 %reduce-scatter.13.cloned.1.call-start = ((), (), s32[]{:S(2)}) async-start(), calls=%async_computation.8 | async-start | bytes 4325376
  113.0 1.6 copy-start.4
  113.0 485.5 %reduce-scatter.15.cloned.1.call-start = ((), (), s32[]{:S(2)}) async-start(), calls=%async_computation.9 | async-start | bytes 4325376
  143.6 8.1 %copy-start.1 = (bf16[1,32,4096]{2,1,0:T(8,128)(2,1)S(1)}, bf16[1,32,4096]{2,1,0:T(8,128)(2,1)}, u32[]{:S(2)}) copy-start(bf16[1,32,4096]{2,1,0:T(8,128)(2,1)} %param.7) | copy-start | bytes 786436
  143.6 8.1 %copy-start.2 = (bf16[1,32,4096]{2,1,0:T(8,128)(2,1)S(1)}, bf16[1,32,4096]{2,1,0:T(8,128)(2,1)}, u32[]{:S(2)}) copy-start(bf16[1,32,4096]{2,1,0:T(8,128)(2,1)} %param.8) | copy-start | bytes 786436
Sparse Core Ops, SparseCore 0:
  9.9 30.6 all-gather.2
  42.4 28.0 all-gather.4
  77.8 36.4 reduce-scatter.10
  116.7 34.9 reduce-scatter.8
  155.4 219.3 reduce-scatter.12
  379.0 219.3 reduce-scatter.14
where the time goes:
time: 610 us; the launch traced here: 607 us
  waiting for transfers between devices  506 us (83%)
  local copies, waits for them, and re-layouts  59.2 us (10%)
  matrix products  22.8 us (4%)
  between operations  16.2 us (3%)
    unnamed x8, waiting for transfers between devices  444 us
    unnamed x21, local copies, waits for them, and re-layouts  56.1 us
    all_gather x1, waiting for transfers between devices, local(): lax.all_gather(tokens, 'block', axis=1, tiled=True)  28 us
    all_gather x1, waiting for transfers between devices, local(): lax.all_gather(cotangent, 'block', axis=1, tiled=True)  25.9 us
  transfers between devices with their start and end apart: 6, of which 5 were waited for; matrix products, arithmetic and copies ran while one was open for 12% of the time, Pallas kernels for 0%

commit v1 on v0

v1 whole, which is shorter than its diff:
```python
import math

import jax
import jax.numpy as jnp
from jax import lax
from jax.experimental import pallas as pl
from jax.experimental.pallas import tpu as pltpu
from jax.sharding import PartitionSpec as P

GELU_C = math.sqrt(2.0 / math.pi)
NX, NZ, NY, NC = 4, 8, 4, 2
BF = jnp.bfloat16
F32 = jnp.float32


def gelu_parts(pre_vals):
    tanh_val = jnp.tanh(GELU_C * (pre_vals + 0.044715 * pre_vals * pre_vals * pre_vals))
    gelu_value = 0.5 * pre_vals * (1.0 + tanh_val)
    gelu_slope = 0.5 * (1.0 + tanh_val) + 0.5 * pre_vals * (1.0 - tanh_val * tanh_val) * GELU_C * (
        1.0 + 3.0 * 0.044715 * pre_vals * pre_vals
    )
    return (gelu_value, gelu_slope)


def to_y(v, k):
    return lax.ppermute(v, "block", [(i, (i + 2 * k) % 8) for i in range(8)])


def to_core(v):
    return lax.ppermute(v, "block", [(i, i ^ 1) for i in range(8)])


def to_x(v, k):
    return lax.ppermute(v, "dp", [(i, ((i // NZ + k) % NX) * NZ + i % NZ) for i in range(NX * NZ)])


def to_z(v, k):
    return lax.ppermute(v, "dp", [(i, (i // NZ) * NZ + (i % NZ + k) % NZ) for i in range(NX * NZ)])


VM = pl.BlockSpec(memory_space=pltpu.VMEM)
SM = pl.BlockSpec(memory_space=pltpu.SMEM)
WSTEP = 256
ORDER = (0, -1, 2, 1)


def call(kernel, ins, outs, flops, moved, scratch=()):
    return pl.pallas_call(
        kernel,
        out_shape=[jax.ShapeDtypeStruct(shape, kind) for shape, kind in outs],
        in_specs=[spec for _, spec in ins],
        out_specs=[VM for _ in outs],
        scratch_shapes=list(scratch),
        compiler_params=pltpu.CompilerParams(vmem_limit_bytes=24 * 1024 * 1024),
        cost_estimate=pl.CostEstimate(flops=1, bytes_accessed=1, transcendentals=0),
    )(*[v for v, _ in ins])


def near(send, v, after=(None, None, None)):
    return [send(then(v, a), k) for k, a in zip((1, 2, -1), after)]


def then(v, after):
    return v if after is None else lax.optimization_barrier((v, after))[0]


def swap_y(v):
    groups = [[2 * y + c for y in range(NY)] for c in range(NC)]
    return lax.all_to_all(v, "block", 0, 0, tiled=True, axis_index_groups=groups)


def dot(a, b, ca, cb):
    return lax.dot_general(a, b, (((ca,), (cb,)), ((), ())), preferred_element_type=F32)


def live(width, at, n, kind):
    limit = WSTEP * width[lax.axis_index("dp")]
    return (at + lax.broadcasted_iota(jnp.int32, (1, n), 1) < limit).astype(F32).astype(kind)


def quarter_kernel(x_ref, dy_ref, width, *outs):
    quarter = x_ref.shape[2] // NX
    x = lax.axis_index("dp") // NZ
    for out, k in zip(outs, (1, 2, -1)):
        at = pl.multiple_of(lax.rem(x + k + NX, NX) * quarter, quarter)
        mask = live(width, at, quarter, BF)
        out[:, :quarter] = x_ref[0, :, pl.ds(at, quarter)] * mask
        out[:, quarter:] = dy_ref[0, :, pl.ds(at, quarter)] * mask


def masked_rows(mine, other, width, at, n):
    at = pl.multiple_of(at, n)
    rows = jnp.concatenate([mine[:, pl.ds(at, n)], other[:, pl.ds(at, n)]], axis=0)
    return rows * live(width, at, n, BF)


def hidden_kernel(mine, other, w1, width, active, hidden, slope, acc):
    n = 1024
    acc[...] = jnp.zeros_like(acc)

    @pl.loop(0, mine.shape[1] // n)
    def _(j):
        at = pl.multiple_of(j * n, n)
        acc[...] += dot(masked_rows(mine, other, width, at, n), w1[0, pl.ds(at, n), :], 1, 0)

    gate = active[lax.axis_index("dp"), lax.axis_index("block")].astype(F32)
    rows = 32

    @pl.loop(0, acc.shape[0] // rows)
    def _(j):
        at = pl.ds(pl.multiple_of(j * rows, rows), rows)
        value, grad = gelu_parts(acc[at, :])
        hidden[at, :] = (value * gate).astype(BF)
        slope[at, :] = grad * gate


def grad_kernel(mine, other, w2, width, slope, grad, acc):
    n = 1024
    acc[...] = jnp.zeros_like(acc)

    @pl.loop(0, mine.shape[1] // n)
    def _(j):
        at = pl.multiple_of(j * n, n)
        acc[...] += dot(masked_rows(mine, other, width, at, n), w2[0, :, pl.ds(at, n)], 1, 1)

    grad[...] = (acc[...] * slope[...]).astype(BF)


def parts_of(rows, hidden, grad, w1, w2, width, at, n):
    mask = live(width, at, n, F32)
    out = dot(hidden[rows, :], w2[0, :, pl.ds(at, n)], 1, 0) * mask
    back = dot(grad[rows, :], w1[0, pl.ds(at, n), :], 1, 1) * mask
    return out, back


def other_kernel(hidden, grad, w1, w2, width, out):
    n, feats = 512, w1.shape[1]
    half = hidden.shape[0] // 2

    @pl.loop(0, feats // n)
    def _(j):
        at = pl.multiple_of(j * n, n)
        a, b = parts_of(pl.ds(half, half), hidden, grad, w1, w2, width, at, n)
        out[:, pl.ds(at, n)] = a.astype(BF)
        out[:, pl.ds(pl.multiple_of(feats + at, n), n)] = b.astype(BF)


def place(k, rows):
    y = lax.axis_index("block") // NC
    return pl.ds(pl.multiple_of(lax.rem(y + k + NY, NY) * rows, rows), rows)


def mine_kernel(hidden, grad, w1, w2, width, got, out):
    n, feats = 512, w1.shape[1]
    half = hidden.shape[0] // 2
    rows = half // 4

    @pl.loop(0, feats // n)
    def _(j):
        at = pl.multiple_of(j * n, n)
        pair = parts_of(pl.ds(0, half), hidden, grad, w1, w2, width, at, n)
        for k, part in enumerate(pair):
            to = pl.ds(pl.multiple_of(k * feats + at, n), n)
            part = (part + got[:, to].astype(F32)).astype(BF)
            for r, k in enumerate(ORDER):
                out[place(k, rows), to] = part[r * rows : (r + 1) * rows]


def terms_kernel(*refs):
    (mx, ox, mdy, ody, me, oe, width), refs = refs[:7], refs[7:]
    hs, gs, (far, up, down, rest), (left, right, acc) = refs[:4], refs[4:8], refs[8:12], refs[12:]
    dp = lax.axis_index("dp")
    x, z = dp // NZ, lax.rem(dp, NZ)
    rows = mx.shape[0]
    part = rows // NY
    quarter = mx.shape[1] // NX
    units = right.shape[1]
    own = pl.ds(pl.multiple_of(x * quarter, quarter), quarter)
    mask = live(width, x * quarter, quarter, BF)
    for which, (mine, other, hid) in enumerate(((mx, ox, gs), (mdy, ody, hs))):
        left[:rows, :] = mine[:, own] * mask
        left[rows : 2 * rows, :] = other[:, own] * mask
        for k in range(3):
            at = (2 * k + which) * quarter
            for half, got in enumerate((me, oe)):
                for r, step in enumerate(ORDER):
                    to = (2 * k + 2 + half) * rows + r * part
                    left[to : to + part, :] = got[place(step, part), at : at + quarter]
        for k in range(4):
            right[2 * k * rows : 2 * (k + 1) * rows, :] = hid[k][...]

        @pl.loop(0, quarter // 256)
        def _(j):
            term = dot(left[:, pl.ds(pl.multiple_of(j * 256, 256), 256)], right[...], 0, 0)
            acc[2 * j, :, which * units : (which + 1) * units] = term[:128]
            acc[2 * j + 1, :, which * units : (which + 1) * units] = term[128:]

    def pick(k):
        return acc[lax.rem(z + k + NZ, NZ)]

    n = acc.shape[1]
    far[...] = pick(4).astype(BF)
    up[:n, :] = pick(3).astype(BF)
    up[n:, :] = pick(1).astype(BF)
    down[:n, :] = pick(-3).astype(BF)
    down[n:, :] = pick(-1).astype(BF)
    for r, k in enumerate((2, -2, 0)):
        rest[r] = pick(k)


def middle_kernel(rest, up, down, low, high, up_far, down_far):
    half = low.shape[0]
    n = 2 * half
    up_far[:half, :] = (rest[0, :half] + up[:half, :].astype(F32) + low[...].astype(F32)).astype(BF)
    up_far[half:, :] = (rest[0, half:] + up[half:n, :].astype(F32)).astype(BF)
    down_far[:half, :] = (rest[1, :half] + down[:half, :].astype(F32)).astype(BF)
    down_far[half:, :] = (rest[1, half:] + down[half:n, :].astype(F32) + high[...].astype(F32)).astype(BF)


def last_kernel(rest, up, down, up_far, down_far, counts, up_grad, down_grad):
    n = rest.shape[1]
    units = up_grad.shape[2]
    scale = 1.0 / counts[lax.axis_index("block")].astype(F32)
    total = rest[2] + up[n:, :].astype(F32) + down[n:, :].astype(F32)
    total = (total + up_far[...].astype(F32) + down_far[...].astype(F32)) * scale
    up_grad[0] = total[:, :units]
    down_grad[0] = total[:, units:].T


def rows_kernel(x, dy, parts, mixed, input_grad):
    rows, feats = x.shape[1:]
    total = sum(parts[k * rows : (k + 1) * rows, :].astype(F32) for k in range(NY))
    mixed[0] = (x[0].astype(F32) + total[:, :feats]).astype(BF)
    input_grad[0] = (dy[0].astype(F32) + total[:, feats:]).astype(BF)


def local(tokens, cotangent, w_up, w_down, active, width, counts):
    rows, feats = tokens.shape[1:]
    units = w_up.shape[2]
    quarter = feats // NX
    v = lambda *arrays: [(array, VM) for array in arrays]
    s = lambda *arrays: [(array, SM) for array in arrays]
    mib = 2**20

    near_x = near(to_y, tokens[0])
    chunks = call(
        quarter_kernel, v(tokens, cotangent) + s(width), [((rows, 2 * quarter), BF)] * 3, 0, mib
    )
    near_dy = near(to_y, cotangent[0], near_x)
    extra = jnp.concatenate([to_x(c, k) for c, k in zip(chunks, (1, 2, -1))], axis=1)
    mine_x = jnp.concatenate([tokens[0]] + near_x, axis=0)
    other_x = to_core(then(mine_x, extra))
    mine_e = swap_y(jnp.concatenate([then(extra, near_dy[0])] * NY, axis=0))
    mine_dy = jnp.concatenate([cotangent[0]] + near_dy, axis=0)
    other_dy = to_core(mine_dy)

    big = 2 * 8 * rows * feats * units
    pair = [((8 * rows, units), BF), ((8 * rows, units), F32)]
    total = pltpu.VMEM((8 * rows, units), F32)
    hidden, slope = call(
        hidden_kernel, v(mine_x, other_x, w_up) + s(width, active), pair, big, 7 * mib, [total]
    )
    hidden_x = [hidden] + near(to_x, hidden)
    other_dy = then(other_dy, (hidden_x[1], hidden_x[3]))
    (grad,) = call(
        grad_kernel, v(mine_dy, other_dy, w_down) + s(width) + v(slope), pair[:1], big, 7 * mib, [total]
    )
    grad_x = [grad] + near(to_x, grad, hidden_x[1:])

    weights = v(hidden, grad, w_up, w_down) + s(width)
    (others,) = call(other_kernel, weights, [((4 * rows, 2 * feats), BF)], big, 10 * mib)
    got = then(to_core(others), hidden_x[2])
    (parts,) = call(mine_kernel, weights + v(got), [((4 * rows, 2 * feats), BF)], big, 12 * mib)
    mixed, input_grad = call(
        rows_kernel, v(tokens, cotangent, swap_y(parts)), [((1, rows, feats), BF)] * 2, 0, 3 * mib
    )
    other_e = to_core(then(mine_e, parts))

    n = quarter // NZ
    far, up, down, rest = call(
        terms_kernel,
        v(mine_x, other_x, mine_dy, other_dy, mine_e, other_e) + s(width) + v(*hidden_x, *grad_x),
        [((n, 2 * units), BF), ((2 * n, 2 * units), BF), ((2 * n, 2 * units), BF), ((3, n, 2 * units), F32)],
        2 * big,
        12 * mib,
        [
            pltpu.VMEM((NX * 8 * rows, quarter), BF),
            pltpu.VMEM((NX * 8 * rows, units), BF),
            pltpu.VMEM((NZ, n, 2 * units), F32),
        ],
    )
    low, high = to_z(far[: n // 2], 2), to_z(far[n // 2 :], -2)
    up, down = to_z(up, 1), to_z(down, -1)
    up_far, down_far = call(
        middle_kernel, v(rest, up, down, low, high), [((n, 2 * units), BF)] * 2, 0, 3 * mib
    )
    up_far, down_far = to_z(up_far, 2), to_z(down_far, -2)
    up_grad, down_grad = call(
        last_kernel,
        v(rest, up, down, up_far, down_far) + s(counts),
        [((1, n, units), F32), ((1, units, n), F32)],
        0,
        3 * mib,
    )
    return (mixed, input_grad, up_grad, down_grad)


def solution(mesh):
    in_specs = (
        P("dp", "block", None),
        P("dp", "block", None),
        P("block", None, None),
        P("block", None, None),
        P(),
        P(),
        P(),
    )
    out_specs = (
        P("dp", "block", None),
        P("dp", "block", None),
        P("block", "dp", None),
        P("block", None, "dp"),
    )
    return jax.shard_map(local, mesh=mesh, in_specs=in_specs, out_specs=out_specs, check_vma=False)
```

time: 610 us -> 167 us (0.27)
  waiting for transfers between devices: 506 us -> 74.1 us
  starting transfers between devices: 0.24 us -> 41.8 us
  local copies, waits for them, and re-layouts: 59.2 us -> 18.8 us
  Pallas kernels: 0 us -> 29.2 us
  matrix products: 22.8 us -> 0 us
  between operations: 16.2 us -> 0.89 us
    unnamed x8 -> x0, waiting for transfers between devices: 444 us -> none
    ppermute x0 -> x25, waiting for transfers between devices: none -> 74.1 us  [the longest x9 36.9 us: to_x(): lax.ppermute(v, 'dp', [(i, (i // NZ + k) % NX * NZ + i % NZ) for i in ran...]
    all_gather x2 -> x0, waiting for transfers between devices: 53.9 us -> none  [the longest x1 28 us: local(): lax.all_gather(tokens, 'block', axis=1, tiled=True)]
    unnamed x21 -> x57, local copies, waits for them, and re-layouts: 56.1 us -> 18.8 us
    ppermute x0 -> x25, starting transfers between devices: none -> 33 us  [the longest x6 12.9 us: to_z(): lax.ppermute(v, 'dp', [(i, i // NZ * NZ + (i % NZ + k) % NZ) for i in ran...]
    pallas_call x0 -> x9, Pallas kernels: none -> 29.2 us  [call(): pl.pallas_call(kernel, out_shape=[jax.ShapeDtypeStruct(shape, kind) for s...]
    dot_general x6 -> x0, matrix products: 22.8 us -> none  [the longest x1 4.98 us: local(): jnp.einsum('bru,bud->brd', hidden, w_down, preferred_element_type=jnp.flo...]
    all_to_all x0 -> x2, starting transfers between devices: none -> 8.79 us  [swap_y(): lax.all_to_all(v, 'block', 0, 0, tiled=True, axis_index_groups=groups)]
  transfers between devices with their start and end apart: 6 -> 27, of which waited for: 5 -> 13; matrix products, arithmetic and copies ran while one was open for 12% -> 1% of each run, Pallas kernels for 0% -> 11%
where the time goes in v1:
time: 167 us; the launch traced here: 166 us
  waiting for transfers between devices  74.1 us (44%)
  starting transfers between devices  41.8 us (25%)
  Pallas kernels  29.2 us (17%)
  local copies, waits for them, and re-layouts  18.8 us (11%)
    ppermute x9, waiting for transfers between devices, to_x(): lax.ppermute(v, 'dp', [(i, (i // NZ + k) % NX * NZ + i % NZ) for i in ran...  36.9 us
    pallas_call x9, Pallas kernels, call(): pl.pallas_call(kernel, out_shape=[jax.ShapeDtypeStruct(shape, kind) for s...  29.2 us
    ppermute x6, waiting for transfers between devices, to_z(): lax.ppermute(v, 'dp', [(i, i // NZ * NZ + (i % NZ + k) % NZ) for i in ran...  24.1 us
    unnamed x57, local copies, waits for them, and re-layouts  18.8 us
    ppermute x6, waiting for transfers between devices, to_y(): return lax.ppermute(v, 'block', [(i, (i + 2 * k) % 8) for i in range(8)])  13.1 us
    ppermute x6, starting transfers between devices, to_z(): lax.ppermute(v, 'dp', [(i, i // NZ * NZ + (i % NZ + k) % NZ) for i in ran...  12.9 us
    ppermute x9, starting transfers between devices, to_x(): lax.ppermute(v, 'dp', [(i, (i // NZ + k) % NX * NZ + i % NZ) for i in ran...  12.3 us
    all_to_all x2, starting transfers between devices, swap_y(): lax.all_to_all(v, 'block', 0, 0, tiled=True, axis_index_groups=groups)  8.79 us
  transfers between devices with their start and end apart: 27, of which 13 were waited for; matrix products, arithmetic and copies ran while one was open for 1% of the time, Pallas kernels for 11%

profile of v1, /device:TPU:6, one launch (start us, length us, event | category | flops | bytes accessed | tf_op | source)
XLA Modules:
  0.0 166.3 jit_solution(6218381902687969570)
XLA Ops:
  9.0 2.4 %collective-permute-start.4 = (bf16[32,2048]{1,0:T(8,128)(2,1)S(1)}, bf16[32,2048]{1,0:T(8,128)(2,1)S(1)}, u32[]{:S(2)}, u32[]{:S(2)}) collective-permute-start(bf16[32,2048]{1,0:T(8,128)(2,1)S(1)} %get-tuple-element.31), channel_id=1, source_target_pairs={{0,128},{8,136},{16,144},{24,152},{32,160},{40,168},{48,176},{56,1... | collective-permute-start | bytes 393224 | tf_op jit(solution)/shard_map/ppermute | solution.py:34
  11.4 5.1 %collective-permute-done.4 = bf16[32,2048]{1,0:T(8,128)(2,1)S(1)} collective-permute-done((bf16[32,2048]{1,0:T(8,128)(2,1)S(1)}, bf16[32,2048]{1,0:T(8,128)(2,1)S(1)}, u32[]{:S(2)}, u32[]{:S(2)}) %collective-permute-start.4) | collective-permute-done | bytes 131104 | tf_op jit(solution)/shard_map/ppermute | solution.py:34
  18.3 3.7 %collective-permute-start.9 = (bf16[32,4096]{1,0:T(8,128)(2,1)S(1)}, bf16[32,4096]{1,0:T(8,128)(2,1)S(1)}, u32[]{:S(2)}, u32[]{:S(2)}) collective-permute-start(bf16[32,4096]{1,0:T(8,128)(2,1)S(1)} %bitcast.11), channel_id=1, source_target_pairs={{0,6},{1,7},{2,0},{3,1},{4,2},{5,3},{6,4},{7,5},{8,14},{9,15},{10,... | collective-permute-start | bytes 786440 | tf_op jit(solution)/shard_map/ppermute | solution.py:26
  23.1 9.0 %collective-permute-done.9 = bf16[32,4096]{1,0:T(8,128)(2,1)S(1)} collective-permute-done((bf16[32,4096]{1,0:T(8,128)(2,1)S(1)}, bf16[32,4096]{1,0:T(8,128)(2,1)S(1)}, u32[]{:S(2)}, u32[]{:S(2)}) %collective-permute-start.9) | collective-permute-done | bytes 262176 | tf_op jit(solution)/shard_map/ppermute | solution.py:26
  32.8 3.1 %collective-permute-done.7 = bf16[32,4096]{1,0:T(8,128)(2,1)S(1)} collective-permute-done((bf16[32,4096]{1,0:T(8,128)(2,1)S(1)}, bf16[32,4096]{1,0:T(8,128)(2,1)S(1)}, u32[]{:S(2)}, u32[]{:S(2)}) %collective-permute-start.7) | collective-permute-done | bytes 262176 | tf_op jit(solution)/shard_map/ppermute | solution.py:26
  36.1 2.3 %copy-done.2 = bf16[1,4096,512]{2,1,0:T(8,128)(2,1)S(1)} copy-done((bf16[1,4096,512]{2,1,0:T(8,128)(2,1)S(1)}, bf16[1,4096,512]{2,1,0:T(8,128)(2,1)}, u32[]{:S(2)}) %copy-start.2) | copy-done | bytes 4194328
  38.5 3.0 %shard_map.103 = (bf16[256,512]{1,0:T(8,128)(2,1)S(1)}, f32[256,512]{1,0:T(8,128)S(1)}) custom-call(bf16[128,4096]{1,0:T(8,128)(2,1)S(1)} %pad_maximum_fusion.1.mine.refs_0_, bf16[128,4096]{1,0:T(8,128)(2,1)S(1)} %collective-permute-done.6.other.refs_1_, bf16[1,4096,512]{2,1,0:T(8,128)(2,1)S(1)} %copy-done.2, s32[32]{0:T(128)S(1)} %copy-done.22, ...), custom_call_target="tpu_custom_call" | custom-call | flops 1 | bytes 1 | tf_op jit(solution)/shard_map/pallas_call | solution.py:48
  42.5 2.4 %collective-permute-start.11 = (bf16[256,512]{1,0:T(8,128)(2,1)S(1)}, bf16[256,512]{1,0:T(8,128)(2,1)S(1)}, u32[]{:S(2)}, u32[]{:S(2)}) collective-permute-start(bf16[256,512]{1,0:T(8,128)(2,1)S(1)} %get-tuple-element.34.hidden.refs_7_), channel_id=1, source_target_pairs={{0,64},{8,72},{16,80},{24,88},{32,96},{40,104},{48,112},{56,120},{... | collective-permute-start | bytes 786440 | tf_op jit(solution)/shard_map/ppermute | solution.py:34
  44.8 6.7 %collective-permute-done.12.refs_10_ = bf16[256,512]{1,0:T(8,128)(2,1)S(1)} collective-permute-done((bf16[256,512]{1,0:T(8,128)(2,1)S(1)}, bf16[256,512]{1,0:T(8,128)(2,1)S(1)}, u32[]{:S(2)}, u32[]{:S(2)}) %collective-permute-start.12) | collective-permute-done | bytes 262176 | tf_op jit(solution)/shard_map/ppermute | solution.py:34
  52.9 3.4 %shard_map.104.grad.refs_11_ = bf16[256,512]{1,0:T(8,128)(2,1)S(1)} custom-call(bf16[128,4096]{1,0:T(8,128)(2,1)S(1)} %pad_maximum_fusion.2.mine.refs_2_, bf16[128,4096]{1,0:T(8,128)(2,1)} %collective-permute-done.10.other.refs_3_, bf16[1,512,4096]{2,1,0:T(8,128)(2,1)S(1)} %copy-done, s32[32]{0:T(128)S(1)} %copy-done.22, f32[256,512]{1,0:T(8,128)S(1)} %get-tuple-element.39.slope), custom_call_target="tpu_custom_call" | custom-call | flops 1 | bytes 1 | tf_op jit(solution)/shard_map/pallas_call | solution.py:48
  56.3 5.1 %shard_map.105 = bf16[128,8192]{1,0:T(8,128)(2,1)} custom-call(bf16[256,512]{1,0:T(8,128)(2,1)S(1)} %get-tuple-element.34.hidden.refs_7_, bf16[256,512]{1,0:T(8,128)(2,1)S(1)} %shard_map.104.grad.refs_11_, bf16[1,4096,512]{2,1,0:T(8,128)(2,1)S(1)} %copy-done.3, bf16[1,512,4096]{2,1,0:T(8,128)(2,1)S(1)} %copy-done, s32[32]{0:T(128)S(1)} %copy-done.22), custom_call_target="tpu_custom_call" | custom-call | flops 1 | bytes 1 | tf_op jit(solution)/shard_map/pallas_call | solution.py:48
  62.8 4.3 %all-to-all-start.1 = ((bf16[4,32,6144]{2,1,0:T(8,128)(2,1)}), bf16[4,32,6144]{2,1,0:T(8,128)(2,1)}, u32[]{:S(2)}, u32[]{:S(2)}) async-start(bf16[4,32,6144]{2,1,0:T(8,128)(2,1)} %bitcast.15), calls=%async_computation.1 | async-start | bytes 3145728 | tf_op jit(solution)/shard_map/all_to_all | solution.py:69
  68.1 9.5 %collective-permute-done.14.refs_9_ = bf16[256,512]{1,0:T(8,128)(2,1)S(1)} collective-permute-done((bf16[256,512]{1,0:T(8,128)(2,1)}, bf16[256,512]{1,0:T(8,128)(2,1)S(1)}, u32[]{:S(2)}, u32[]{:S(2)}) %collective-permute-start.14) | collective-permute-done | bytes 262176 | tf_op jit(solution)/shard_map/ppermute | solution.py:34
  83.7 4.8 %shard_map.106 = bf16[128,8192]{1,0:T(8,128)(2,1)S(1)} custom-call(bf16[256,512]{1,0:T(8,128)(2,1)S(1)} %copy-done.9, bf16[256,512]{1,0:T(8,128)(2,1)S(1)} %shard_map.104.grad.refs_11_, bf16[1,4096,512]{2,1,0:T(8,128)(2,1)S(1)} %copy-done.4, bf16[1,512,4096]{2,1,0:T(8,128)(2,1)S(1)} %copy-done.1, s32[32]{0:T(128)S(1)} %copy-done.22, ...), custom_call_target="tpu_custom_call" | custom-call | flops 1 | bytes 1 | tf_op jit(solution)/shard_map/pallas_call | solution.py:48
  89.9 4.4 %all-to-all-start = ((bf16[4,32,8192]{2,1,0:T(8,128)(2,1)}), bf16[4,32,8192]{2,1,0:T(8,128)(2,1)}, u32[]{:S(2)}, u32[]{:S(2)}) async-start(bf16[4,32,8192]{2,1,0:T(8,128)(2,1)} %bitcast.6), calls=%async_computation | async-start | bytes 4194304 | tf_op jit(solution)/shard_map/all_to_all | solution.py:69
  97.6 10.9 %collective-permute-done.16.refs_12_ = bf16[256,512]{1,0:T(8,128)(2,1)S(1)} collective-permute-done((bf16[256,512]{1,0:T(8,128)(2,1)S(1)}, bf16[256,512]{1,0:T(8,128)(2,1)S(1)}, u32[]{:S(2)}, u32[]{:S(2)}) %collective-permute-start.16) | collective-permute-done | bytes 262176 | tf_op jit(solution)/shard_map/ppermute | solution.py:34
  108.5 3.4 %collective-permute-done.18.refs_14_ = bf16[256,512]{1,0:T(8,128)(2,1)S(1)} collective-permute-done((bf16[256,512]{1,0:T(8,128)(2,1)S(1)}, bf16[256,512]{1,0:T(8,128)(2,1)S(1)}, u32[]{:S(2)}, u32[]{:S(2)}) %collective-permute-start.18) | collective-permute-done | bytes 262176 | tf_op jit(solution)/shard_map/ppermute | solution.py:34
  115.7 6.7 %shard_map.108 = (bf16[128,1024]{1,0:T(8,128)(2,1)S(1)}, bf16[256,1024]{1,0:T(8,128)(2,1)S(1)}, bf16[256,1024]{1,0:T(8,128)(2,1)S(1)}, f32[3,128,1024]{2,1,0:T(8,128)S(1)}) custom-call(bf16[128,4096]{1,0:T(8,128)(2,1)S(1)} %pad_maximum_fusion.1.mine.refs_0_, bf16[128,4096]{1,0:T(8,128)(2,1)S(1)} %collective-permute-done.6.other.refs_1_, ...), custom_call_target="tpu_custom_call" | custom-call | flops 1 | bytes 1 | tf_op jit(solution)/shard_map/pallas_call | solution.py:48
  123.2 4.0 %collective-permute-start.20 = (bf16[256,1024]{1,0:T(8,128)(2,1)S(1)}, bf16[256,1024]{1,0:T(8,128)(2,1)S(1)}, u32[]{:S(2)}, u32[]{:S(2)}) collective-permute-start(bf16[256,1024]{1,0:T(8,128)(2,1)S(1)} %get-tuple-element.50), channel_id=1, source_target_pairs={{0,56},{8,0},{16,8},{24,16},{32,24},{40,32},{48,40},{56,48},{64,12... | collective-permute-start | bytes 1572872 | tf_op jit(solution)/shard_map/ppermute | solution.py:38
  127.2 2.5 %collective-permute-start.22 = (bf16[64,1024]{1,0:T(8,128)(2,1)S(1)}, bf16[64,1024]{1,0:T(8,128)(2,1)S(1)}, u32[]{:S(2)}, u32[]{:S(2)}) collective-permute-start(bf16[64,1024]{1,0:T(8,128)(2,1)S(1)} %get-tuple-element.56), channel_id=1, source_target_pairs={{0,48},{8,56},{16,0},{24,8},{32,16},{40,24},{48,32},{56,40},{64,11... | collective-permute-start | bytes 393224 | tf_op jit(solution)/shard_map/ppermute | solution.py:38
  130.2 14.1 %collective-permute-done.22.high = bf16[64,1024]{1,0:T(8,128)(2,1)S(1)} collective-permute-done((bf16[64,1024]{1,0:T(8,128)(2,1)S(1)}, bf16[64,1024]{1,0:T(8,128)(2,1)S(1)}, u32[]{:S(2)}, u32[]{:S(2)}) %collective-permute-start.22) | collective-permute-done | bytes 131104 | tf_op jit(solution)/shard_map/ppermute | solution.py:38
  146.4 5.2 %collective-permute-start.23 = (bf16[128,1024]{1,0:T(8,128)(2,1)}, bf16[128,1024]{1,0:T(8,128)(2,1)S(1)}, u32[]{:S(2)}, u32[]{:S(2)}) collective-permute-start(bf16[128,1024]{1,0:T(8,128)(2,1)} %get-tuple-element.52), channel_id=1, source_target_pairs={{0,16},{8,24},{16,32},{24,40},{32,48},{40,56},{48,0},{56,8},{64,80... | collective-permute-start | bytes 786440 | tf_op jit(solution)/shard_map/ppermute | solution.py:38
  151.6 2.7 %shard_map.107 = (bf16[1,32,4096]{2,1,0:T(8,128)(2,1)}, bf16[1,32,4096]{2,1,0:T(8,128)(2,1)}) custom-call(bf16[1,32,4096]{2,1,0:T(8,128)(2,1)S(1)} %copy-done.12, bf16[1,32,4096]{2,1,0:T(8,128)(2,1)S(1)} %copy-done.14, bf16[128,8192]{1,0:T(8,128)(2,1)} %bitcast.3.parts), custom_call_target="tpu_custom_call" | custom-call | flops 1 | bytes 1 | tf_op jit(solution)/shard_map/pallas_call | solution.py:48
  154.3 8.1 %collective-permute-done.23.up_far = bf16[128,1024]{1,0:T(8,128)(2,1)S(1)} collective-permute-done((bf16[128,1024]{1,0:T(8,128)(2,1)}, bf16[128,1024]{1,0:T(8,128)(2,1)S(1)}, u32[]{:S(2)}, u32[]{:S(2)}) %collective-permute-start.23) | collective-permute-done | bytes 262176 | tf_op jit(solution)/shard_map/ppermute | solution.py:38
  (101 shorter events, 38.5 us)
Async XLA Ops:
  6.1 12.2 %collective-permute-start.2 = (bf16[32,4096]{1,0:T(8,128)(2,1)S(1)}, bf16[32,4096]{1,0:T(8,128)(2,1)S(1)}, u32[]{:S(2)}, u32[]{:S(2)}) collective-permute-start(bf16[32,4096]{1,0:T(8,128)(2,1)S(1)} %bitcast.7), channel_id=1, source_target_pairs={{0,6},{1,7},{2,0},{3,1},{4,2},{5,3},{6,4},{7,5},{8,14},{9,15},{10,... | collective-permute-start | bytes 786440 | tf_op jit(solution)/shard_map/ppermute | solution.py:26
  7.4 14.6 %collective-permute-start.1 = (bf16[32,4096]{1,0:T(8,128)(2,1)S(1)}, bf16[32,4096]{1,0:T(8,128)(2,1)S(1)}, u32[]{:S(2)}, u32[]{:S(2)}) collective-permute-start(bf16[32,4096]{1,0:T(8,128)(2,1)S(1)} %bitcast.8), channel_id=1, source_target_pairs={{0,4},{1,5},{2,6},{3,7},{4,0},{5,1},{6,2},{7,3},{8,12},{9,13},{10,... | collective-permute-start | bytes 786440 | tf_op jit(solution)/shard_map/ppermute | solution.py:26
  8.0 14.0 %collective-permute-start = (bf16[32,4096]{1,0:T(8,128)(2,1)S(1)}, bf16[32,4096]{1,0:T(8,128)(2,1)S(1)}, u32[]{:S(2)}, u32[]{:S(2)}) collective-permute-start(bf16[32,4096]{1,0:T(8,128)(2,1)S(1)} %bitcast.9), channel_id=1, source_target_pairs={{0,2},{1,3},{2,4},{3,5},{4,6},{5,7},{6,0},{7,1},{8,10},{9,11},{10,... | collective-permute-start | bytes 786440 | tf_op jit(solution)/shard_map/ppermute | solution.py:26
  18.3 13.8 %collective-permute-start.9 = (bf16[32,4096]{1,0:T(8,128)(2,1)S(1)}, bf16[32,4096]{1,0:T(8,128)(2,1)S(1)}, u32[]{:S(2)}, u32[]{:S(2)}) collective-permute-start(bf16[32,4096]{1,0:T(8,128)(2,1)S(1)} %bitcast.11), channel_id=1, source_target_pairs={{0,6},{1,7},{2,0},{3,1},{4,2},{5,3},{6,4},{7,5},{8,14},{9,15},{10,... | collective-permute-start | bytes 786440 | tf_op jit(solution)/shard_map/ppermute | solution.py:26
  22.0 10.8 %collective-permute-start.8 = (bf16[32,4096]{1,0:T(8,128)(2,1)S(1)}, bf16[32,4096]{1,0:T(8,128)(2,1)S(1)}, u32[]{:S(2)}, u32[]{:S(2)}) collective-permute-start(bf16[32,4096]{1,0:T(8,128)(2,1)S(1)} %bitcast.12), channel_id=1, source_target_pairs={{0,4},{1,5},{2,6},{3,7},{4,0},{5,1},{6,2},{7,3},{8,12},{9,13},{10,... | collective-permute-start | bytes 786440 | tf_op jit(solution)/shard_map/ppermute | solution.py:26
  22.0 13.8 %collective-permute-start.7 = (bf16[32,4096]{1,0:T(8,128)(2,1)S(1)}, bf16[32,4096]{1,0:T(8,128)(2,1)S(1)}, u32[]{:S(2)}, u32[]{:S(2)}) collective-permute-start(bf16[32,4096]{1,0:T(8,128)(2,1)S(1)} %bitcast.13), channel_id=1, source_target_pairs={{0,2},{1,3},{2,4},{3,5},{4,6},{5,7},{6,0},{7,1},{8,10},{9,11},{10,... | collective-permute-start | bytes 786440 | tf_op jit(solution)/shard_map/ppermute | solution.py:26
  23.0 13.1 %collective-permute-start.6 = (bf16[128,4096]{1,0:T(8,128)(2,1)S(1)}, bf16[128,4096]{1,0:T(8,128)(2,1)S(1)}, u32[]{:S(2)}, u32[]{:S(2)}) collective-permute-start(bf16[128,4096]{1,0:T(8,128)(2,1)S(1)} %pad_maximum_fusion.1.mine.refs_0_), channel_id=1, source_target_pairs={{0,1},{1,0},{2,3},{3,2},{4,5},{5,4},{6,7},{7,6},{8,9},{9,8},{10,11... | collective-permute-start | bytes 3145736 | tf_op jit(solution)/shard_map/ppermute | solution.py:30
  35.9 8.9 %collective-permute-start.10 = (bf16[128,4096]{1,0:T(8,128)(2,1)S(1)}, bf16[128,4096]{1,0:T(8,128)(2,1)}, u32[]{:S(2)}, u32[]{:S(2)}) collective-permute-start(bf16[128,4096]{1,0:T(8,128)(2,1)S(1)} %pad_maximum_fusion.2.mine.refs_2_), channel_id=1, source_target_pairs={{0,1},{1,0},{2,3},{3,2},{4,5},{5,4},{6,7},{7,6},{8,9},{9,8},{10,11... | collective-permute-start | bytes 3145736 | tf_op jit(solution)/shard_map/ppermute | solution.py:30
  41.5 10.0 %collective-permute-start.12 = (bf16[256,512]{1,0:T(8,128)(2,1)S(1)}, bf16[256,512]{1,0:T(8,128)(2,1)S(1)}, u32[]{:S(2)}, u32[]{:S(2)}) collective-permute-start(bf16[256,512]{1,0:T(8,128)(2,1)S(1)} %get-tuple-element.34.hidden.refs_7_), channel_id=1, source_target_pairs={{0,192},{8,200},{16,208},{24,216},{32,224},{40,232},{48,240},{56,2... | collective-permute-start | bytes 786440 | tf_op jit(solution)/shard_map/ppermute | solution.py:34
  42.5 9.7 %collective-permute-start.11 = (bf16[256,512]{1,0:T(8,128)(2,1)S(1)}, bf16[256,512]{1,0:T(8,128)(2,1)S(1)}, u32[]{:S(2)}, u32[]{:S(2)}) collective-permute-start(bf16[256,512]{1,0:T(8,128)(2,1)S(1)} %get-tuple-element.34.hidden.refs_7_), channel_id=1, source_target_pairs={{0,64},{8,72},{16,80},{24,88},{32,96},{40,104},{48,112},{56,120},{... | collective-permute-start | bytes 786440 | tf_op jit(solution)/shard_map/ppermute | solution.py:34
  61.5 16.9 %collective-permute-start.13 = (bf16[128,8192]{1,0:T(8,128)(2,1)}, bf16[128,8192]{1,0:T(8,128)(2,1)}, u32[]{:S(2)}, u32[]{:S(2)}) collective-permute-start(bf16[128,8192]{1,0:T(8,128)(2,1)} %shard_map.105), channel_id=1, source_target_pairs={{0,1},{1,0},{2,3},{3,2},{4,5},{5,4},{6,7},{7,6},{8,9},{9,8},{10,11... | collective-permute-start | bytes 6291464 | tf_op jit(solution)/shard_map/ppermute | solution.py:30
  62.8 27.1 %all-to-all-start.1 = ((bf16[4,32,6144]{2,1,0:T(8,128)(2,1)}), bf16[4,32,6144]{2,1,0:T(8,128)(2,1)}, u32[]{:S(2)}, u32[]{:S(2)}) async-start(bf16[4,32,6144]{2,1,0:T(8,128)(2,1)} %bitcast.15), calls=%async_computation.1 | async-start | bytes 3145728 | tf_op jit(solution)/shard_map/all_to_all | solution.py:69
  67.1 10.5 %collective-permute-start.14 = (bf16[256,512]{1,0:T(8,128)(2,1)}, bf16[256,512]{1,0:T(8,128)(2,1)S(1)}, u32[]{:S(2)}, u32[]{:S(2)}) collective-permute-start(bf16[256,512]{1,0:T(8,128)(2,1)} %copy-done.8), channel_id=1, source_target_pairs={{0,128},{8,136},{16,144},{24,152},{32,160},{40,168},{48,176},{56,1... | collective-permute-start | bytes 786440 | tf_op jit(solution)/shard_map/ppermute | solution.py:34
  89.9 22.1 %collective-permute-start.15 = (bf16[128,6144]{1,0:T(8,128)(2,1)}, bf16[128,6144]{1,0:T(8,128)(2,1)}, u32[]{:S(2)}, u32[]{:S(2)}) collective-permute-start(bf16[128,6144]{1,0:T(8,128)(2,1)} %bitcast.5.refs_4_), channel_id=1, source_target_pairs={{0,1},{1,0},{2,3},{3,2},{4,5},{5,4},{6,7},{7,6},{8,9},{9,8},{10,11... | collective-permute-start | bytes 4718600 | tf_op jit(solution)/shard_map/ppermute | solution.py:30
  89.9 61.7 %all-to-all-start = ((bf16[4,32,8192]{2,1,0:T(8,128)(2,1)}), bf16[4,32,8192]{2,1,0:T(8,128)(2,1)}, u32[]{:S(2)}, u32[]{:S(2)}) async-start(bf16[4,32,8192]{2,1,0:T(8,128)(2,1)} %bitcast.6), calls=%async_computation | async-start | bytes 4194304 | tf_op jit(solution)/shard_map/all_to_all | solution.py:69
  94.3 14.2 %collective-permute-start.16 = (bf16[256,512]{1,0:T(8,128)(2,1)S(1)}, bf16[256,512]{1,0:T(8,128)(2,1)S(1)}, u32[]{:S(2)}, u32[]{:S(2)}) collective-permute-start(bf16[256,512]{1,0:T(8,128)(2,1)S(1)} %shard_map.104.grad.refs_11_), channel_id=1, source_target_pairs={{0,64},{8,72},{16,80},{24,88},{32,96},{40,104},{48,112},{56,120},{... | collective-permute-start | bytes 786440 | tf_op jit(solution)/shard_map/ppermute | solution.py:34
  96.7 11.9 %collective-permute-start.17 = (bf16[256,512]{1,0:T(8,128)(2,1)S(1)}, bf16[256,512]{1,0:T(8,128)(2,1)S(1)}, u32[]{:S(2)}, u32[]{:S(2)}) collective-permute-start(bf16[256,512]{1,0:T(8,128)(2,1)S(1)} %shard_map.104.grad.refs_11_), channel_id=1, source_target_pairs={{0,128},{8,136},{16,144},{24,152},{32,160},{40,168},{48,176},{56,1... | collective-permute-start | bytes 786440 | tf_op jit(solution)/shard_map/ppermute | solution.py:34
  96.7 15.3 %collective-permute-start.18 = (bf16[256,512]{1,0:T(8,128)(2,1)S(1)}, bf16[256,512]{1,0:T(8,128)(2,1)S(1)}, u32[]{:S(2)}, u32[]{:S(2)}) collective-permute-start(bf16[256,512]{1,0:T(8,128)(2,1)S(1)} %shard_map.104.grad.refs_11_), channel_id=1, source_target_pairs={{0,192},{8,200},{16,208},{24,216},{32,224},{40,232},{48,240},{56,2... | collective-permute-start | bytes 786440 | tf_op jit(solution)/shard_map/ppermute | solution.py:34
  122.5 21.8 %collective-permute-start.19 = (bf16[256,1024]{1,0:T(8,128)(2,1)S(1)}, bf16[256,1024]{1,0:T(8,128)(2,1)S(1)}, u32[]{:S(2)}, u32[]{:S(2)}) collective-permute-start(bf16[256,1024]{1,0:T(8,128)(2,1)S(1)} %get-tuple-element.49), channel_id=1, source_target_pairs={{0,8},{8,16},{16,24},{24,32},{32,40},{40,48},{48,56},{56,0},{64,72... | collective-permute-start | bytes 1572872 | tf_op jit(solution)/shard_map/ppermute | solution.py:38
  123.2 21.1 %collective-permute-start.20 = (bf16[256,1024]{1,0:T(8,128)(2,1)S(1)}, bf16[256,1024]{1,0:T(8,128)(2,1)S(1)}, u32[]{:S(2)}, u32[]{:S(2)}) collective-permute-start(bf16[256,1024]{1,0:T(8,128)(2,1)S(1)} %get-tuple-element.50), channel_id=1, source_target_pairs={{0,56},{8,0},{16,8},{24,16},{32,24},{40,32},{48,40},{56,48},{64,12... | collective-permute-start | bytes 1572872 | tf_op jit(solution)/shard_map/ppermute | solution.py:38
  127.2 17.1 %collective-permute-start.22 = (bf16[64,1024]{1,0:T(8,128)(2,1)S(1)}, bf16[64,1024]{1,0:T(8,128)(2,1)S(1)}, u32[]{:S(2)}, u32[]{:S(2)}) collective-permute-start(bf16[64,1024]{1,0:T(8,128)(2,1)S(1)} %get-tuple-element.56), channel_id=1, source_target_pairs={{0,48},{8,56},{16,0},{24,8},{32,16},{40,24},{48,32},{56,40},{64,11... | collective-permute-start | bytes 393224 | tf_op jit(solution)/shard_map/ppermute | solution.py:38
  129.7 14.6 %collective-permute-start.21 = (bf16[64,1024]{1,0:T(8,128)(2,1)S(1)}, bf16[64,1024]{1,0:T(8,128)(2,1)S(1)}, u32[]{:S(2)}, u32[]{:S(2)}) collective-permute-start(bf16[64,1024]{1,0:T(8,128)(2,1)S(1)} %get-tuple-element.57), channel_id=1, source_target_pairs={{0,16},{8,24},{16,32},{24,40},{32,48},{40,56},{48,0},{56,8},{64,80... | collective-permute-start | bytes 393224 | tf_op jit(solution)/shard_map/ppermute | solution.py:38
  146.4 16.0 %collective-permute-start.23 = (bf16[128,1024]{1,0:T(8,128)(2,1)}, bf16[128,1024]{1,0:T(8,128)(2,1)S(1)}, u32[]{:S(2)}, u32[]{:S(2)}) collective-permute-start(bf16[128,1024]{1,0:T(8,128)(2,1)} %get-tuple-element.52), channel_id=1, source_target_pairs={{0,16},{8,24},{16,32},{24,40},{32,48},{40,56},{48,0},{56,8},{64,80... | collective-permute-start | bytes 786440 | tf_op jit(solution)/shard_map/ppermute | solution.py:38
  151.6 12.7 %collective-permute-start.24 = (bf16[128,1024]{1,0:T(8,128)(2,1)}, bf16[128,1024]{1,0:T(8,128)(2,1)}, u32[]{:S(2)}, u32[]{:S(2)}) collective-permute-start(bf16[128,1024]{1,0:T(8,128)(2,1)} %get-tuple-element.53), channel_id=1, source_target_pairs={{0,48},{8,56},{16,0},{24,8},{32,16},{40,24},{48,32},{56,40},{64,11... | collective-permute-start | bytes 786440 | tf_op jit(solution)/shard_map/ppermute | solution.py:38
  (30 other events, 216.4 us)

commit v2 on v1

v2 whole, which is shorter than its diff:
```python
import math

import jax
import jax.numpy as jnp
from jax import lax
from jax.experimental import pallas as pl
from jax.experimental.pallas import tpu as pltpu
from jax.sharding import PartitionSpec as P

GELU_C = math.sqrt(2.0 / math.pi)
NX, NZ, NY, NC = 4, 8, 4, 2
BF = jnp.bfloat16
F32 = jnp.float32


def gelu_parts(pre_vals):
    tanh_val = jnp.tanh(GELU_C * (pre_vals + 0.044715 * pre_vals * pre_vals * pre_vals))
    gelu_value = 0.5 * pre_vals * (1.0 + tanh_val)
    gelu_slope = 0.5 * (1.0 + tanh_val) + 0.5 * pre_vals * (1.0 - tanh_val * tanh_val) * GELU_C * (
        1.0 + 3.0 * 0.044715 * pre_vals * pre_vals
    )
    return (gelu_value, gelu_slope)


def to_y(v, k):
    return lax.ppermute(v, "block", [(i, (i + 2 * k) % 8) for i in range(8)])


def to_core(v):
    return lax.ppermute(v, "block", [(i, i ^ 1) for i in range(8)])


def to_x(v, k):
    return lax.ppermute(v, "dp", [(i, ((i // NZ + k) % NX) * NZ + i % NZ) for i in range(NX * NZ)])


def to_z(v, k):
    return lax.ppermute(v, "dp", [(i, (i // NZ) * NZ + (i % NZ + k) % NZ) for i in range(NX * NZ)])


VM = pl.BlockSpec(memory_space=pltpu.VMEM)
HB = pl.BlockSpec(memory_space=pl.ANY)
SM = pl.BlockSpec(memory_space=pltpu.SMEM)
WSTEP = 256


def call(kernel, ins, outs, scratch=(), mib=24):
    return pl.pallas_call(
        kernel,
        out_shape=[jax.ShapeDtypeStruct(shape, kind) for shape, kind in outs],
        in_specs=[spec for _, spec in ins],
        out_specs=[VM for _ in outs],
        scratch_shapes=list(scratch),
        compiler_params=pltpu.CompilerParams(vmem_limit_bytes=mib * 2**20),
        cost_estimate=pl.CostEstimate(flops=1, bytes_accessed=1, transcendentals=0),
    )(*[v for v, _ in ins])


def fetch(sources, sems):
    copies = [pltpu.make_async_copy(a, b, sems.at[k]) for k, (a, b) in enumerate(sources)]
    for copy in copies:
        copy.start()
    return copies


def near(send, v, after=(None, None, None)):
    return [send(then(v, a), k) for k, a in zip((1, 2, -1), after)]


def ring(send, v):
    half = v.shape[0] // 2
    before, after = send(v, 1), send(v, -1)
    return [before, send(before[:half], 1), send(after[half:], -1), after]


def then(v, after):
    return v if after is None else lax.optimization_barrier((v, after))[0]


def dot(a, b, ca, cb):
    return lax.dot_general(a, b, (((ca,), (cb,)), ((), ())), preferred_element_type=F32)


def live(width, at, n, kind):
    limit = WSTEP * width[lax.axis_index("dp")]
    return (at + lax.broadcasted_iota(jnp.int32, (1, n), 1) < limit).astype(F32).astype(kind)


def quarter_kernel(x_ref, dy_ref, width, a, b, c, x_own, dy_own, sems):
    for copy in fetch([(x_ref.at[0], x_own), (dy_ref.at[0], dy_own)], sems):
        copy.wait()
    quarter = x_own.shape[1] // NX
    x = lax.axis_index("dp") // NZ
    for out, k in zip((a, b, c), (1, 2, -1)):
        at = pl.multiple_of(lax.rem(x + k + NX, NX) * quarter, quarter)
        mask = live(width, at, quarter, BF)
        out[:, :quarter] = x_own[:, pl.ds(at, quarter)] * mask
        out[:, quarter:] = dy_own[:, pl.ds(at, quarter)] * mask


def masked_rows(mine, other, width, at, n):
    rows = jnp.concatenate([mine[:, at : at + n], other[:, at : at + n]], axis=0)
    return rows * live(width, at, n, BF)


CHUNKS = 4


def hidden_kernel(mine, other, w1, width, active, hidden, slope, held, sems):
    n = mine.shape[1] // CHUNKS
    cuts = [j * n for j in range(CHUNKS)]
    copies = fetch([(w1.at[0, pl.ds(at, n), :], held.at[pl.ds(at, n), :]) for at in cuts], sems)
    pre = 0.0
    for at, copy in zip(cuts, copies):
        copy.wait()
        pre += dot(masked_rows(mine, other, width, at, n), held[at : at + n, :], 1, 0)
    slope[...] = pre
    gate = active[lax.axis_index("block"), lax.axis_index("dp")].astype(F32)
    rows = 32

    @pl.loop(0, slope.shape[0] // rows)
    def _(j):
        at = pl.ds(pl.multiple_of(j * rows, rows), rows)
        value, grad = gelu_parts(slope[at, :])
        hidden[at, :] = (value * gate).astype(BF)
        slope[at, :] = grad * gate


def grad_kernel(mine, other, w2, width, hidden, slope, both, held, sems):
    n = mine.shape[1] // CHUNKS
    units = hidden.shape[1]
    cuts = [j * n for j in range(CHUNKS)]
    copies = fetch([(w2.at[0, :, pl.ds(at, n)], held.at[:, pl.ds(at, n)]) for at in cuts], sems)
    both[:, :units] = hidden[...]
    back = 0.0
    for at, copy in zip(cuts, copies):
        copy.wait()
        back += dot(masked_rows(mine, other, width, at, n), held[:, at : at + n], 1, 1)
    both[:, units:] = (back * slope[...]).astype(BF)


def out_kernel(hidden, w2, width, out, held, sems):
    n = out.shape[1] // CHUNKS
    cuts = [j * n for j in range(CHUNKS)]
    copies = fetch([(w2.at[0, :, pl.ds(at, n)], held.at[:, pl.ds(at, n)]) for at in cuts], sems)
    for at, copy in zip(cuts, copies):
        copy.wait()
        part = dot(hidden[...], held[:, at : at + n], 1, 0) * live(width, at, n, F32)
        out[:, at : at + n] = part.astype(BF)


def in_kernel(both, w1, out, width, mine, other, held, sems):
    feats, units = w1.shape[1:]
    n = feats // CHUNKS
    half = mine.shape[0]
    cuts = [j * n for j in range(CHUNKS)]
    copies = fetch([(w1.at[0, pl.ds(at, n), :], held.at[pl.ds(at, n), :]) for at in cuts], sems)
    mine[:, :feats] = out[:half, :]
    other[:, :feats] = out[half:, :]
    for at, copy in zip(cuts, copies):
        copy.wait()
        part = dot(both[:, units:], held[at : at + n, :], 1, 1) * live(width, at, n, F32)
        mine[:, feats + at : feats + at + n] = part[:half].astype(BF)
        other[:, feats + at : feats + at + n] = part[half:].astype(BF)


def pair_kernel(mine, got, *outs):
    rows = mine.shape[0] // NY
    for r, out in enumerate(outs):
        at = slice(r * rows, (r + 1) * rows)
        out[...] = (mine[at, :].astype(F32) + got[at, :].astype(F32)).astype(BF)


def pass_kernel(before, after, low, high, before_out, after_out):
    half = low.shape[0]
    after_out[:half, :] = (after[:half, :].astype(F32) + low[...].astype(F32)).astype(BF)
    after_out[half:, :] = after[half:, :]
    before_out[:half, :] = before[:half, :]
    before_out[half:, :] = (before[half:, :].astype(F32) + high[...].astype(F32)).astype(BF)


def terms_kernel(*refs):
    ins, width, hgs, refs = refs[:6], refs[6], refs[7:12], refs[12:]
    far, up, down, mid, own, left, right, acc, sems = refs
    dp = lax.axis_index("dp")
    x, z = dp // NZ, lax.rem(dp, NZ)
    rows = ins[0].shape[0]
    quarter = ins[0].shape[1] // NX
    units = right.shape[2]
    at = pl.ds(pl.multiple_of(x * quarter, quarter), quarter)
    jobs = []
    for which, (mine, other) in enumerate(((ins[2], ins[3]), (ins[0], ins[1]))):
        jobs += [
            (mine.at[:, at], left.at[which, pl.ds(0, rows), :]),
            (other.at[:, at], left.at[which, pl.ds(rows, rows), :]),
        ]
        for k in range(3):
            cut = pl.ds((2 * k + 1 - which) * quarter, quarter)
            for half in range(2):
                to = pl.ds((2 * k + 2 + half) * rows, rows)
                jobs.append((ins[4 + half].at[:, cut], left.at[which, to, :]))
        to = 0
        for piece in hgs:
            n = piece.shape[0]
            cols = pl.ds(which * units, units)
            jobs.append((piece.at[:, cols], right.at[which, pl.ds(to, n), :]))
            to += n
    copies = fetch(jobs, sems)
    mask = live(width, x * quarter, quarter, BF)
    count = len(copies) // 2
    for which in range(2):
        for copy in copies[which * count : (which + 1) * count]:
            copy.wait()
        left[which, : 2 * rows, :] = left[which, : 2 * rows, :] * mask
        col = (1 - which) * units
        for j in range(quarter // 512):
            term = dot(left[which, :, j * 512 : (j + 1) * 512], right[which], 0, 0)
            for k in range(4):
                acc[4 * j + k, :, col : col + units] = term[128 * k : 128 * (k + 1)]

    def pick(k):
        return acc[lax.rem(z + k + NZ, NZ)]

    n = acc.shape[1]
    far[...] = pick(4).astype(BF)
    up[:n, :] = pick(3).astype(BF)
    up[n:, :] = pick(1).astype(BF)
    down[:n, :] = pick(-3).astype(BF)
    down[n:, :] = pick(-1).astype(BF)
    mid[0] = pick(2)
    mid[1] = pick(-2)
    own[...] = pick(0)


def middle_kernel(mid, up, down, low, high, up_far, down_far):
    half = low.shape[0]
    n = 2 * half
    up_far[:half, :] = (mid[0, :half] + up[:half, :].astype(F32) + low[...].astype(F32)).astype(BF)
    up_far[half:, :] = (mid[0, half:] + up[half:n, :].astype(F32)).astype(BF)
    down_far[:half, :] = (mid[1, :half] + down[:half, :].astype(F32)).astype(BF)
    down_far[half:, :] = (mid[1, half:] + down[half:n, :].astype(F32) + high[...].astype(F32)).astype(BF)


def last_kernel(own, up, down, up_far, down_far, counts, up_grad, down_grad):
    n = own.shape[0]
    units = up_grad.shape[2]
    scale = 1.0 / counts[lax.axis_index("block")].astype(F32)
    total = own[...] + up[n:, :].astype(F32) + down[n:, :].astype(F32)
    total = (total + up_far[...].astype(F32) + down_far[...].astype(F32)) * scale
    up_grad[0] = total[:, :units]
    down_grad[0] = total[:, units:].T


def rows_kernel(x, dy, own, below, above, mixed, input_grad):
    feats = x.shape[2]
    total = own[...].astype(F32) + below[...].astype(F32) + above[...].astype(F32)
    mixed[0] = (x[0].astype(F32) + total[:, :feats]).astype(BF)
    input_grad[0] = (dy[0].astype(F32) + total[:, feats:]).astype(BF)


def local(tokens, cotangent, w_up, w_down, active, width, counts):
    rows, feats = tokens.shape[1:]
    units = w_up.shape[2]
    quarter = feats // NX
    n = quarter // NZ
    v = lambda *arrays: [(array, VM) for array in arrays]
    h = lambda *arrays: [(array, HB) for array in arrays]
    s = lambda *arrays: [(array, SM) for array in arrays]
    sems = lambda k: pltpu.SemaphoreType.DMA((k,))

    together = lambda *arrays: lax.optimization_barrier(arrays)

    pair = jnp.concatenate([tokens[0], cotangent[0]], axis=0)
    near_b = near(to_y, pair)
    chunks = call(
        quarter_kernel,
        h(tokens, cotangent) + s(width),
        [((rows, 2 * quarter), BF)] * 3,
        [pltpu.VMEM((rows, feats), BF)] * 2 + [sems(2)],
        56,
    )
    swapped = [to_x(c, k) for c, k in zip(chunks, (1, 2, -1))]
    pair, *got = together(pair, *swapped, *near_b)
    extra, near_b = jnp.concatenate(got[:3], axis=1), got[3:]

    mine_x = jnp.concatenate([b[:rows] for b in [pair] + near_b], axis=0)
    other_x = to_core(mine_x)
    mine_dy = jnp.concatenate([b[rows:] for b in [pair] + near_b], axis=0)
    other_dy = to_core(mine_dy)
    before, after = to_y(extra, 1), to_y(extra, -1)
    held_up = pltpu.VMEM((feats, units), BF)
    held_down = pltpu.VMEM((units, feats), BF)
    hidden, slope = call(
        hidden_kernel,
        v(mine_x, other_x) + h(w_up) + s(width, active.T),
        [((8 * rows, units), BF), ((8 * rows, units), F32)],
        [held_up, sems(CHUNKS)],
        50,
    )
    (out,) = call(
        out_kernel,
        v(hidden) + h(w_down) + s(width),
        [((8 * rows, feats), BF)],
        [held_down, sems(CHUNKS)],
        24,
    )
    hidden, slope, other_dy, before, after, out = together(
        hidden, slope, other_dy, before, after, out
    )

    (both,) = call(
        grad_kernel,
        v(mine_dy, other_dy) + h(w_down) + s(width) + v(hidden, slope),
        [((8 * rows, 2 * units), BF)],
        [held_down, sems(CHUNKS)],
        24,
    )
    left, right = to_x(both, 1), to_x(both, -1)
    half = rows // 2
    far = [to_y(before[:half], 1), to_y(after[half:], -1)]
    mine_e = jnp.concatenate([extra, before, *far, after], axis=0)
    mine, other = call(
        in_kernel,
        v(both) + h(w_up) + v(out) + s(width),
        [((4 * rows, 2 * feats), BF)] * 2,
        [held_up, sems(CHUNKS)],
        24,
    )
    both, left, right, mine_e, mine, other = together(both, left, right, mine_e, mine, other)

    both_x = [left, to_x(left[: 4 * rows], 1), to_x(right[4 * rows :], -1), right]
    other_e = to_core(mine_e)
    got = to_core(other)
    parts = call(pair_kernel, v(mine, got), [((rows, 2 * feats), BF)] * 4)
    both_x[1], both_x[2], other_e, *parts = together(both_x[1], both_x[2], other_e, *parts)
    sum_own, sum_before, sum_far, sum_after = parts
    sum_low, sum_high = to_y(sum_far[:half], 1), to_y(sum_far[half:], -1)

    far, up, down, mid, own = call(
        terms_kernel,
        h(mine_x, other_x, mine_dy, other_dy, mine_e, other_e) + s(width) + h(both, *both_x),
        [((n, 2 * units), BF), ((2 * n, 2 * units), BF), ((2 * n, 2 * units), BF)]
        + [((2, n, 2 * units), F32), ((n, 2 * units), F32)],
        [
            pltpu.VMEM((2, NX * 8 * rows, quarter), BF),
            pltpu.VMEM((2, NX * 8 * rows, units), BF),
            pltpu.VMEM((NZ, n, 2 * units), F32),
            sems(26),
        ],
    )
    far, sum_low, sum_high = together(far, sum_low, sum_high)
    low, high = to_z(far[: n // 2], 2), to_z(far[n // 2 :], -2)
    up, down = to_z(up, 1), to_z(down, -1)
    low, high, up, down = together(low, high, up, down)
    up_far, down_far = call(
        middle_kernel, v(mid, up, down, low, high), [((n, 2 * units), BF)] * 2
    )
    up_far, down_far = to_z(up_far, 2), to_z(down_far, -2)
    up_grad, down_grad = call(
        last_kernel,
        v(own, up, down, up_far, down_far) + s(counts),
        [((1, n, units), F32), ((1, units, n), F32)],
    )
    sum_before, sum_after = call(
        pass_kernel, v(sum_before, sum_after, sum_low, sum_high), [((rows, 2 * feats), BF)] * 2
    )
    mixed, input_grad = call(
        rows_kernel, v(tokens, cotangent, sum_own, to_y(sum_after, 1), to_y(sum_before, -1)), [((1, rows, feats), BF)] * 2
    )
    return (mixed, input_grad, up_grad, down_grad)


def solution(mesh):
    in_specs = (
        P("dp", "block", None),
        P("dp", "block", None),
        P("block", None, None),
        P("block", None, None),
        P(),
        P(),
        P(),
    )
    out_specs = (
        P("dp", "block", None),
        P("dp", "block", None),
        P("block", "dp", None),
        P("block", None, "dp"),
    )
    return jax.shard_map(local, mesh=mesh, in_specs=in_specs, out_specs=out_specs, check_vma=False)
```

time: 167 us -> 120 us (0.72)
  waiting for transfers between devices: 74.1 us -> 54.5 us
  local copies, waits for them, and re-layouts: 18.8 us -> 0.48 us
  Pallas kernels: 29.2 us -> 22.7 us
    ppermute x9 -> x7, waiting for transfers between devices: 36.9 us -> 16.4 us  [to_x(): lax.ppermute(v, 'dp', [(i, (i // NZ + k) % NX * NZ + i % NZ) for i in ran...]
    unnamed x57 -> x20, local copies, waits for them, and re-layouts: 18.8 us -> 0.15 us
    ppermute x6 -> x11, starting transfers between devices: 7.51 us -> 19.2 us  [to_y(): return lax.ppermute(v, 'block', [(i, (i + 2 * k) % 8) for i in range(8)])]
    all_to_all x2 -> x0, starting transfers between devices: 8.79 us -> none  [swap_y(): lax.all_to_all(v, 'block', 0, 0, tiled=True, axis_index_groups=groups)]
    pallas_call x9 -> x11, Pallas kernels: 29.2 us -> 22.7 us  [call(): pl.pallas_call(kernel, out_shape=[jax.ShapeDtypeStruct(shape, kind) for s...]
    ppermute x9 -> x7, starting transfers between devices: 12.3 us -> 8.5 us  [to_x(): lax.ppermute(v, 'dp', [(i, (i // NZ + k) % NX * NZ + i % NZ) for i in ran...]
    ppermute x6 -> x11, waiting for transfers between devices: 13.1 us -> 11.9 us  [to_y(): return lax.ppermute(v, 'block', [(i, (i + 2 * k) % 8) for i in range(8)])]
  transfers between devices with their start and end apart: 27 -> 28, of which waited for: 13 -> 14; matrix products, arithmetic and copies ran while one was open for 1% -> 0% of each run, Pallas kernels for 11% -> 15%
where the time goes in v2:
time: 120 us
  waiting for transfers between devices  54.5 us (45%)
  starting transfers between devices  40.5 us (34%)
  Pallas kernels  22.7 us (19%)
  other arithmetic  1.23 us (1%)
    ppermute x6, waiting for transfers between devices, to_z(): lax.ppermute(v, 'dp', [(i, i // NZ * NZ + (i % NZ + k) % NZ) for i in ran...  24.9 us
    pallas_call x11, Pallas kernels, call(): pl.pallas_call(kernel, out_shape=[jax.ShapeDtypeStruct(shape, kind) for s...  22.7 us
    ppermute x11, starting transfers between devices, to_y(): return lax.ppermute(v, 'block', [(i, (i + 2 * k) % 8) for i in range(8)])  19.2 us
    ppermute x7, waiting for transfers between devices, to_x(): lax.ppermute(v, 'dp', [(i, (i // NZ + k) % NX * NZ + i % NZ) for i in ran...  16.4 us
    ppermute x11, waiting for transfers between devices, to_y(): return lax.ppermute(v, 'block', [(i, (i + 2 * k) % 8) for i in range(8)])  11.9 us
    ppermute x6, starting transfers between devices, to_z(): lax.ppermute(v, 'dp', [(i, i // NZ * NZ + (i % NZ + k) % NZ) for i in ran...  11.6 us
    ppermute x7, starting transfers between devices, to_x(): lax.ppermute(v, 'dp', [(i, (i // NZ + k) % NX * NZ + i % NZ) for i in ran...  8.5 us
  transfers between devices with their start and end apart: 28, of which 14 were waited for; matrix products, arithmetic and copies ran while one was open for 0% of the time, Pallas kernels for 15%

profile of v2, /device:TPU:6, one launch (start us, length us, event | category | flops | bytes accessed | tf_op | source)
XLA Modules:
  0.0 120.3 jit_solution(6365519210980531521)
XLA Ops:
  3.4 2.9 %collective-permute-start.4 = (bf16[64,4096]{1,0:T(8,128)(2,1)S(1)}, bf16[64,4096]{1,0:T(8,128)(2,1)S(1)}, u32[]{:S(2)}, u32[]{:S(2)}) collective-permute-start(bf16[64,4096]{1,0:T(8,128)(2,1)S(1)} %pad_maximum_fusion.2), channel_id=1, source_target_pairs={{0,4},{1,5},{2,6},{3,7},{4,0},{5,1},{6,2},{7,3},{8,12},{9,13},{10,... | collective-permute-start | bytes 1572872 | tf_op jit(solution)/shard_map/ppermute | solution.py:26
  7.6 2.5 %shard_map.102 = (bf16[32,2048]{1,0:T(8,128)(2,1)}, bf16[32,2048]{1,0:T(8,128)(2,1)}, bf16[32,2048]{1,0:T(8,128)(2,1)}) custom-call(bf16[1,32,4096]{2,1,0:T(8,128)(2,1)} %x.1, bf16[1,32,4096]{2,1,0:T(8,128)(2,1)} %dy.1, s32[32]{0:T(128)} %refs_6_.1), custom_call_target="tpu_custom_call" | custom-call | flops 1 | bytes 1 | tf_op jit(solution)/shard_map/pallas_call | solution.py:48
  10.6 2.4 %collective-permute-start.1 = (bf16[32,2048]{1,0:T(8,128)(2,1)}, bf16[32,2048]{1,0:T(8,128)(2,1)S(1)}, u32[]{:S(2)}, u32[]{:S(2)}) collective-permute-start(bf16[32,2048]{1,0:T(8,128)(2,1)} %get-tuple-element.62), channel_id=1, source_target_pairs={{0,128},{8,136},{16,144},{24,152},{32,160},{40,168},{48,176},{56,1... | collective-permute-start | bytes 393224 | tf_op jit(solution)/shard_map/ppermute | solution.py:34
  13.1 3.1 %collective-permute-done = bf16[32,2048]{1,0:T(8,128)(2,1)S(1)} collective-permute-done((bf16[32,2048]{1,0:T(8,128)(2,1)}, bf16[32,2048]{1,0:T(8,128)(2,1)S(1)}, u32[]{:S(2)}, u32[]{:S(2)}) %collective-permute-start) | collective-permute-done | bytes 131104 | tf_op jit(solution)/shard_map/ppermute | solution.py:34
  17.4 5.1 %collective-permute-done.2 = bf16[32,2048]{1,0:T(8,128)(2,1)S(1)} collective-permute-done((bf16[32,2048]{1,0:T(8,128)(2,1)}, bf16[32,2048]{1,0:T(8,128)(2,1)S(1)}, u32[]{:S(2)}, u32[]{:S(2)}) %collective-permute-start.2) | collective-permute-done | bytes 131104 | tf_op jit(solution)/shard_map/ppermute | solution.py:34
  22.6 6.6 %collective-permute-done.4 = bf16[64,4096]{1,0:T(8,128)(2,1)S(1)} collective-permute-done((bf16[64,4096]{1,0:T(8,128)(2,1)S(1)}, bf16[64,4096]{1,0:T(8,128)(2,1)S(1)}, u32[]{:S(2)}, u32[]{:S(2)}) %collective-permute-start.4) | collective-permute-done | bytes 524320 | tf_op jit(solution)/shard_map/ppermute | solution.py:26
  31.6 2.0 %collective-permute-start.9 = (bf16[32,6144]{1,0:T(8,128)(2,1)S(1)}, bf16[32,6144]{1,0:T(8,128)(2,1)S(1)}, u32[]{:S(2)}, u32[]{:S(2)}) collective-permute-start(bf16[32,6144]{1,0:T(8,128)(2,1)S(1)} %get-tuple-element.131), channel_id=1, source_target_pairs={{0,6},{1,7},{2,0},{3,1},{4,2},{5,3},{6,4},{7,5},{8,14},{9,15},{10,... | collective-permute-start | bytes 1179656 | tf_op jit(solution)/shard_map/ppermute | solution.py:26
  33.6 4.3 %shard_map.103 = (bf16[256,512]{1,0:T(8,128)(2,1)S(1)}, f32[256,512]{1,0:T(8,128)S(1)}) custom-call(bf16[128,4096]{1,0:T(8,128)(2,1)S(1)} %pad_maximum_fusion.1.mine.refs_0_, bf16[128,4096]{1,0:T(8,128)(2,1)S(1)} %collective-permute-done.6.other.refs_1_, bf16[1,4096,512]{2,1,0:T(8,128)(2,1)} %w1.3, s32[32]{0:T(128)S(1)} %copy-done.4, s32[8,32]{1,0:T(8,128)S(1)} %bitcast.5), custom_call_target="tpu_custom_call" | custom-call | flops 1 | bytes 1 | tf_op jit(solution)/shard_map/pallas_call | solution.py:48
  37.9 2.9 %shard_map.104.out = bf16[256,4096]{1,0:T(8,128)(2,1)S(1)} custom-call(bf16[256,512]{1,0:T(8,128)(2,1)S(1)} %get-tuple-element.74.hidden, bf16[1,512,4096]{2,1,0:T(8,128)(2,1)S(1)} %copy-done.1, s32[32]{0:T(128)S(1)} %copy-done.4), custom_call_target="tpu_custom_call" | custom-call | flops 1 | bytes 1 | tf_op jit(solution)/shard_map/pallas_call | solution.py:48
  42.6 2.7 %shard_map.105.both.refs_7_ = bf16[256,1024]{1,0:T(8,128)(2,1)S(1)} custom-call(bf16[128,4096]{1,0:T(8,128)(2,1)S(1)} %pad_maximum_fusion.mine.refs_2_, bf16[128,4096]{1,0:T(8,128)(2,1)S(1)} %collective-permute-done.7.other.refs_3_, bf16[1,512,4096]{2,1,0:T(8,128)(2,1)S(1)} %copy-done.1, s32[32]{0:T(128)S(1)} %copy-done.4, ...), custom_call_target="tpu_custom_call" | custom-call | flops 1 | bytes 1 | tf_op jit(solution)/shard_map/pallas_call | solution.py:48
  48.6 2.9 %shard_map.106 = (bf16[128,8192]{1,0:T(8,128)(2,1)S(1)}, bf16[128,8192]{1,0:T(8,128)(2,1)S(1)}) custom-call(bf16[256,1024]{1,0:T(8,128)(2,1)S(1)} %shard_map.105.both.refs_7_, bf16[1,4096,512]{2,1,0:T(8,128)(2,1)S(1)} %copy-done, bf16[256,4096]{1,0:T(8,128)(2,1)S(1)} %shard_map.104.out, s32[32]{0:T(128)S(1)} %copy-done.4), custom_call_target="tpu_custom_call" | custom-call | flops 1 | bytes 1 | tf_op jit(solution)/shard_map/pallas_call | solution.py:48
  51.6 2.3 %collective-permute-start.13 = (bf16[16,6144]{1,0:T(8,128)(2,1)S(1)}, bf16[16,6144]{1,0:T(8,128)(2,1)S(1)}, u32[]{:S(2)}, u32[]{:S(2)}) collective-permute-start(bf16[16,6144]{1,0:T(8,128)(2,1)S(1)} %slice.57), channel_id=1, source_target_pairs={{0,6},{1,7},{2,0},{3,1},{4,2},{5,3},{6,4},{7,5},{8,14},{9,15},{10,... | collective-permute-start | bytes 589832 | tf_op jit(solution)/shard_map/ppermute | solution.py:26
  54.5 2.8 %collective-permute-done.13 = bf16[16,6144]{1,0:T(8,128)(2,1)S(1)} collective-permute-done((bf16[16,6144]{1,0:T(8,128)(2,1)S(1)}, bf16[16,6144]{1,0:T(8,128)(2,1)S(1)}, u32[]{:S(2)}, u32[]{:S(2)}) %collective-permute-start.13) | collective-permute-done | bytes 196640 | tf_op jit(solution)/shard_map/ppermute | solution.py:26
  60.8 1.9 %collective-permute-start.15 = (bf16[128,1024]{1,0:T(8,128)(2,1)S(1)}, bf16[128,1024]{1,0:T(8,128)(2,1)S(1)}, u32[]{:S(2)}, u32[]{:S(2)}) collective-permute-start(bf16[128,1024]{1,0:T(8,128)(2,1)S(1)} %slice.59), channel_id=1, source_target_pairs={{0,192},{8,200},{16,208},{24,216},{32,224},{40,232},{48,240},{56,2... | collective-permute-start | bytes 786440 | tf_op jit(solution)/shard_map/ppermute | solution.py:34
  64.6 4.2 %collective-permute-done.14.refs_9_ = bf16[128,1024]{1,0:T(8,128)(2,1)S(1)} collective-permute-done((bf16[128,1024]{1,0:T(8,128)(2,1)S(1)}, bf16[128,1024]{1,0:T(8,128)(2,1)S(1)}, u32[]{:S(2)}, u32[]{:S(2)}) %collective-permute-start.14) | collective-permute-done | bytes 262176 | tf_op jit(solution)/shard_map/ppermute | solution.py:34
  70.9 2.5 %collective-permute-start.19 = (bf16[16,8192]{1,0:T(8,128)(2,1)S(1)}, bf16[16,8192]{1,0:T(8,128)(2,1)S(1)}, u32[]{:S(2)}, u32[]{:S(2)}) collective-permute-start(bf16[16,8192]{1,0:T(8,128)(2,1)S(1)} %get-tuple-element.118), channel_id=1, source_target_pairs={{0,6},{1,7},{2,0},{3,1},{4,2},{5,3},{6,4},{7,5},{8,14},{9,15},{10,... | collective-permute-start | bytes 786440 | tf_op jit(solution)/shard_map/ppermute | solution.py:26
  73.5 4.1 %shard_map.108 = (bf16[128,1024]{1,0:T(8,128)(2,1)S(1)}, bf16[256,1024]{1,0:T(8,128)(2,1)S(1)}, bf16[256,1024]{1,0:T(8,128)(2,1)S(1)}, f32[2,128,1024]{2,1,0:T(8,128)S(1)}, f32[128,1024]{1,0:T(8,128)S(1)}) custom-call(bf16[128,4096]{1,0:T(8,128)(2,1)S(1)} %pad_maximum_fusion.1.mine.refs_0_, bf16[128,4096]{1,0:T(8,128)(2,1)S(1)} %collective-permute-done.6.other.refs_1_, ...), custom_call_target="tpu_custom_call" | custom-call | flops 1 | bytes 1 | tf_op jit(solution)/shard_map/pallas_call | solution.py:48
  77.6 2.0 %collective-permute-start.24 = (bf16[256,1024]{1,0:T(8,128)(2,1)S(1)}, bf16[256,1024]{1,0:T(8,128)(2,1)S(1)}, u32[]{:S(2)}, u32[]{:S(2)}) collective-permute-start(bf16[256,1024]{1,0:T(8,128)(2,1)S(1)} %get-tuple-element.107), channel_id=1, source_target_pairs={{0,8},{8,16},{16,24},{24,32},{32,40},{40,48},{48,56},{56,0},{64,72... | collective-permute-start | bytes 1572872 | tf_op jit(solution)/shard_map/ppermute | solution.py:38
  79.6 4.2 %collective-permute-start.25 = (bf16[256,1024]{1,0:T(8,128)(2,1)S(1)}, bf16[256,1024]{1,0:T(8,128)(2,1)S(1)}, u32[]{:S(2)}, u32[]{:S(2)}) collective-permute-start(bf16[256,1024]{1,0:T(8,128)(2,1)S(1)} %get-tuple-element.108), channel_id=1, source_target_pairs={{0,56},{8,0},{16,8},{24,16},{32,24},{40,32},{48,40},{56,48},{64,12... | collective-permute-start | bytes 1572872 | tf_op jit(solution)/shard_map/ppermute | solution.py:38
  84.2 3.2 %collective-permute-start.21 = (bf16[32,8192]{1,0:T(8,128)(2,1)S(1)}, bf16[32,8192]{1,0:T(8,128)(2,1)S(1)}, u32[]{:S(2)}, u32[]{:S(2)}) collective-permute-start(bf16[32,8192]{1,0:T(8,128)(2,1)S(1)} %get-tuple-element.102), channel_id=1, source_target_pairs={{0,6},{1,7},{2,0},{3,1},{4,2},{5,3},{6,4},{7,5},{8,14},{9,15},{10,... | collective-permute-start | bytes 1572872 | tf_op jit(solution)/shard_map/ppermute | solution.py:26
  87.5 12.2 %collective-permute-done.22.low = bf16[64,1024]{1,0:T(8,128)(2,1)S(1)} collective-permute-done((bf16[64,1024]{1,0:T(8,128)(2,1)S(1)}, bf16[64,1024]{1,0:T(8,128)(2,1)S(1)}, u32[]{:S(2)}, u32[]{:S(2)}) %collective-permute-start.22) | collective-permute-done | bytes 131104 | tf_op jit(solution)/shard_map/ppermute | solution.py:38
  100.8 6.4 %collective-permute-done.23.high = bf16[64,1024]{1,0:T(8,128)(2,1)S(1)} collective-permute-done((bf16[64,1024]{1,0:T(8,128)(2,1)S(1)}, bf16[64,1024]{1,0:T(8,128)(2,1)S(1)}, u32[]{:S(2)}, u32[]{:S(2)}) %collective-permute-start.23) | collective-permute-done | bytes 131104 | tf_op jit(solution)/shard_map/ppermute | solution.py:38
  107.5 4.1 %collective-permute-start.27 = (bf16[128,1024]{1,0:T(8,128)(2,1)S(1)}, bf16[128,1024]{1,0:T(8,128)(2,1)S(1)}, u32[]{:S(2)}, u32[]{:S(2)}) collective-permute-start(bf16[128,1024]{1,0:T(8,128)(2,1)S(1)} %get-tuple-element.115), channel_id=1, source_target_pairs={{0,48},{8,56},{16,0},{24,8},{32,16},{40,24},{48,32},{56,40},{64,11... | collective-permute-start | bytes 786440 | tf_op jit(solution)/shard_map/ppermute | solution.py:38
  112.6 6.2 %collective-permute-done.26.up_far = bf16[128,1024]{1,0:T(8,128)(2,1)S(1)} collective-permute-done((bf16[128,1024]{1,0:T(8,128)(2,1)S(1)}, bf16[128,1024]{1,0:T(8,128)(2,1)S(1)}, u32[]{:S(2)}, u32[]{:S(2)}) %collective-permute-start.26) | collective-permute-done | bytes 262176 | tf_op jit(solution)/shard_map/ppermute | solution.py:38
  (75 shorter events, 25.7 us)
Async XLA Ops:
  1.7 20.9 %collective-permute-start.3 = (bf16[64,4096]{1,0:T(8,128)(2,1)S(1)}, bf16[64,4096]{1,0:T(8,128)(2,1)S(1)}, u32[]{:S(2)}, u32[]{:S(2)}) collective-permute-start(bf16[64,4096]{1,0:T(8,128)(2,1)S(1)} %pad_maximum_fusion.2), channel_id=1, source_target_pairs={{0,2},{1,3},{2,4},{3,5},{4,6},{5,7},{6,0},{7,1},{8,10},{9,11},{10,... | collective-permute-start | bytes 1572872 | tf_op jit(solution)/shard_map/ppermute | solution.py:26
  3.4 25.8 %collective-permute-start.4 = (bf16[64,4096]{1,0:T(8,128)(2,1)S(1)}, bf16[64,4096]{1,0:T(8,128)(2,1)S(1)}, u32[]{:S(2)}, u32[]{:S(2)}) collective-permute-start(bf16[64,4096]{1,0:T(8,128)(2,1)S(1)} %pad_maximum_fusion.2), channel_id=1, source_target_pairs={{0,4},{1,5},{2,6},{3,7},{4,0},{5,1},{6,2},{7,3},{8,12},{9,13},{10,... | collective-permute-start | bytes 1572872 | tf_op jit(solution)/shard_map/ppermute | solution.py:26
  6.3 22.9 %collective-permute-start.5 = (bf16[64,4096]{1,0:T(8,128)(2,1)S(1)}, bf16[64,4096]{1,0:T(8,128)(2,1)S(1)}, u32[]{:S(2)}, u32[]{:S(2)}) collective-permute-start(bf16[64,4096]{1,0:T(8,128)(2,1)S(1)} %pad_maximum_fusion.2), channel_id=1, source_target_pairs={{0,6},{1,7},{2,0},{3,1},{4,2},{5,3},{6,4},{7,5},{8,14},{9,15},{10,... | collective-permute-start | bytes 1572872 | tf_op jit(solution)/shard_map/ppermute | solution.py:26
  10.6 6.8 %collective-permute-start.1 = (bf16[32,2048]{1,0:T(8,128)(2,1)}, bf16[32,2048]{1,0:T(8,128)(2,1)S(1)}, u32[]{:S(2)}, u32[]{:S(2)}) collective-permute-start(bf16[32,2048]{1,0:T(8,128)(2,1)} %get-tuple-element.62), channel_id=1, source_target_pairs={{0,128},{8,136},{16,144},{24,152},{32,160},{40,168},{48,176},{56,1... | collective-permute-start | bytes 393224 | tf_op jit(solution)/shard_map/ppermute | solution.py:34
  16.2 6.4 %collective-permute-start.2 = (bf16[32,2048]{1,0:T(8,128)(2,1)}, bf16[32,2048]{1,0:T(8,128)(2,1)S(1)}, u32[]{:S(2)}, u32[]{:S(2)}) collective-permute-start(bf16[32,2048]{1,0:T(8,128)(2,1)} %get-tuple-element.63), channel_id=1, source_target_pairs={{0,192},{8,200},{16,208},{24,216},{32,224},{40,232},{48,240},{56,2... | collective-permute-start | bytes 393224 | tf_op jit(solution)/shard_map/ppermute | solution.py:34
  29.6 13.0 %collective-permute-start.7 = (bf16[128,4096]{1,0:T(8,128)(2,1)S(1)}, bf16[128,4096]{1,0:T(8,128)(2,1)S(1)}, u32[]{:S(2)}, u32[]{:S(2)}) collective-permute-start(bf16[128,4096]{1,0:T(8,128)(2,1)S(1)} %pad_maximum_fusion.mine.refs_2_), channel_id=1, source_target_pairs={{0,1},{1,0},{2,3},{3,2},{4,5},{5,4},{6,7},{7,6},{8,9},{9,8},{10,11... | collective-permute-start | bytes 3145736 | tf_op jit(solution)/shard_map/ppermute | solution.py:30
  30.3 12.3 %collective-permute-start.8 = (bf16[32,6144]{1,0:T(8,128)(2,1)S(1)}, bf16[32,6144]{1,0:T(8,128)(2,1)S(1)}, u32[]{:S(2)}, u32[]{:S(2)}) collective-permute-start(bf16[32,6144]{1,0:T(8,128)(2,1)S(1)} %get-tuple-element.131), channel_id=1, source_target_pairs={{0,2},{1,3},{2,4},{3,5},{4,6},{5,7},{6,0},{7,1},{8,10},{9,11},{10,... | collective-permute-start | bytes 1179656 | tf_op jit(solution)/shard_map/ppermute | solution.py:26
  31.6 11.0 %collective-permute-start.9 = (bf16[32,6144]{1,0:T(8,128)(2,1)S(1)}, bf16[32,6144]{1,0:T(8,128)(2,1)S(1)}, u32[]{:S(2)}, u32[]{:S(2)}) collective-permute-start(bf16[32,6144]{1,0:T(8,128)(2,1)S(1)} %get-tuple-element.131), channel_id=1, source_target_pairs={{0,6},{1,7},{2,0},{3,1},{4,2},{5,3},{6,4},{7,5},{8,14},{9,15},{10,... | collective-permute-start | bytes 1179656 | tf_op jit(solution)/shard_map/ppermute | solution.py:26
  45.4 13.1 %collective-permute-start.10 = (bf16[256,1024]{1,0:T(8,128)(2,1)S(1)}, bf16[256,1024]{1,0:T(8,128)(2,1)S(1)}, u32[]{:S(2)}, u32[]{:S(2)}) collective-permute-start(bf16[256,1024]{1,0:T(8,128)(2,1)S(1)} %shard_map.105.both.refs_7_), channel_id=1, source_target_pairs={{0,64},{8,72},{16,80},{24,88},{32,96},{40,104},{48,112},{56,120},{... | collective-permute-start | bytes 1572872 | tf_op jit(solution)/shard_map/ppermute | solution.py:34
  45.9 14.0 %collective-permute-start.11 = (bf16[256,1024]{1,0:T(8,128)(2,1)S(1)}, bf16[256,1024]{1,0:T(8,128)(2,1)S(1)}, u32[]{:S(2)}, u32[]{:S(2)}) collective-permute-start(bf16[256,1024]{1,0:T(8,128)(2,1)S(1)} %shard_map.105.both.refs_7_), channel_id=1, source_target_pairs={{0,192},{8,200},{16,208},{24,216},{32,224},{40,232},{48,240},{56,2... | collective-permute-start | bytes 1572872 | tf_op jit(solution)/shard_map/ppermute | solution.py:34
  47.5 7.0 %collective-permute-start.12 = (bf16[16,6144]{1,0:T(8,128)(2,1)S(1)}, bf16[16,6144]{1,0:T(8,128)(2,1)S(1)}, u32[]{:S(2)}, u32[]{:S(2)}) collective-permute-start(bf16[16,6144]{1,0:T(8,128)(2,1)S(1)} %slice.56), channel_id=1, source_target_pairs={{0,2},{1,3},{2,4},{3,5},{4,6},{5,7},{6,0},{7,1},{8,10},{9,11},{10,... | collective-permute-start | bytes 589832 | tf_op jit(solution)/shard_map/ppermute | solution.py:26
  60.0 10.2 %collective-permute-start.16 = (bf16[128,6144]{1,0:T(8,128)(2,1)S(1)}, bf16[128,6144]{1,0:T(8,128)(2,1)S(1)}, u32[]{:S(2)}, u32[]{:S(2)}) collective-permute-start(bf16[128,6144]{1,0:T(8,128)(2,1)S(1)} %constant_dynamic-update-slice_fusion.3.refs_4_), channel_id=1, source_target_pairs={{0,1},{1,0},{2,3},{3,2},{4,5},{5,4},{6,7},{7,6},{8,9},{9,8},{10,11... | collective-permute-start | bytes 4718600 | tf_op jit(solution)/shard_map/ppermute | solution.py:30
  60.5 8.3 %collective-permute-start.14 = (bf16[128,1024]{1,0:T(8,128)(2,1)S(1)}, bf16[128,1024]{1,0:T(8,128)(2,1)S(1)}, u32[]{:S(2)}, u32[]{:S(2)}) collective-permute-start(bf16[128,1024]{1,0:T(8,128)(2,1)S(1)} %slice.58), channel_id=1, source_target_pairs={{0,64},{8,72},{16,80},{24,88},{32,96},{40,104},{48,112},{56,120},{... | collective-permute-start | bytes 786440 | tf_op jit(solution)/shard_map/ppermute | solution.py:34
  60.8 9.3 %collective-permute-start.15 = (bf16[128,1024]{1,0:T(8,128)(2,1)S(1)}, bf16[128,1024]{1,0:T(8,128)(2,1)S(1)}, u32[]{:S(2)}, u32[]{:S(2)}) collective-permute-start(bf16[128,1024]{1,0:T(8,128)(2,1)S(1)} %slice.59), channel_id=1, source_target_pairs={{0,192},{8,200},{16,208},{24,216},{32,224},{40,232},{48,240},{56,2... | collective-permute-start | bytes 786440 | tf_op jit(solution)/shard_map/ppermute | solution.py:34
  70.1 13.7 %collective-permute-start.18 = (bf16[16,8192]{1,0:T(8,128)(2,1)S(1)}, bf16[16,8192]{1,0:T(8,128)(2,1)S(1)}, u32[]{:S(2)}, u32[]{:S(2)}) collective-permute-start(bf16[16,8192]{1,0:T(8,128)(2,1)S(1)} %get-tuple-element.119), channel_id=1, source_target_pairs={{0,2},{1,3},{2,4},{3,5},{4,6},{5,7},{6,0},{7,1},{8,10},{9,11},{10,... | collective-permute-start | bytes 786440 | tf_op jit(solution)/shard_map/ppermute | solution.py:26
  70.9 12.9 %collective-permute-start.19 = (bf16[16,8192]{1,0:T(8,128)(2,1)S(1)}, bf16[16,8192]{1,0:T(8,128)(2,1)S(1)}, u32[]{:S(2)}, u32[]{:S(2)}) collective-permute-start(bf16[16,8192]{1,0:T(8,128)(2,1)S(1)} %get-tuple-element.118), channel_id=1, source_target_pairs={{0,6},{1,7},{2,0},{3,1},{4,2},{5,3},{6,4},{7,5},{8,14},{9,15},{10,... | collective-permute-start | bytes 786440 | tf_op jit(solution)/shard_map/ppermute | solution.py:26
  77.6 29.6 %collective-permute-start.24 = (bf16[256,1024]{1,0:T(8,128)(2,1)S(1)}, bf16[256,1024]{1,0:T(8,128)(2,1)S(1)}, u32[]{:S(2)}, u32[]{:S(2)}) collective-permute-start(bf16[256,1024]{1,0:T(8,128)(2,1)S(1)} %get-tuple-element.107), channel_id=1, source_target_pairs={{0,8},{8,16},{16,24},{24,32},{32,40},{40,48},{48,56},{56,0},{64,72... | collective-permute-start | bytes 1572872 | tf_op jit(solution)/shard_map/ppermute | solution.py:38
  79.6 27.6 %collective-permute-start.25 = (bf16[256,1024]{1,0:T(8,128)(2,1)S(1)}, bf16[256,1024]{1,0:T(8,128)(2,1)S(1)}, u32[]{:S(2)}, u32[]{:S(2)}) collective-permute-start(bf16[256,1024]{1,0:T(8,128)(2,1)S(1)} %get-tuple-element.108), channel_id=1, source_target_pairs={{0,56},{8,0},{16,8},{24,16},{32,24},{40,32},{48,40},{56,48},{64,12... | collective-permute-start | bytes 1572872 | tf_op jit(solution)/shard_map/ppermute | solution.py:38
  83.9 15.8 %collective-permute-start.22 = (bf16[64,1024]{1,0:T(8,128)(2,1)S(1)}, bf16[64,1024]{1,0:T(8,128)(2,1)S(1)}, u32[]{:S(2)}, u32[]{:S(2)}) collective-permute-start(bf16[64,1024]{1,0:T(8,128)(2,1)S(1)} %get-tuple-element.129), channel_id=1, source_target_pairs={{0,16},{8,24},{16,32},{24,40},{32,48},{40,56},{48,0},{56,8},{64,80... | collective-permute-start | bytes 393224 | tf_op jit(solution)/shard_map/ppermute | solution.py:38
  84.1 27.5 %collective-permute-start.20 = (bf16[32,8192]{1,0:T(8,128)(2,1)S(1)}, bf16[32,8192]{1,0:T(8,128)(2,1)S(1)}, u32[]{:S(2)}, u32[]{:S(2)}) collective-permute-start(bf16[32,8192]{1,0:T(8,128)(2,1)S(1)} %get-tuple-element.101), channel_id=1, source_target_pairs={{0,2},{1,3},{2,4},{3,5},{4,6},{5,7},{6,0},{7,1},{8,10},{9,11},{10,... | collective-permute-start | bytes 1572872 | tf_op jit(solution)/shard_map/ppermute | solution.py:26
  84.2 27.4 %collective-permute-start.21 = (bf16[32,8192]{1,0:T(8,128)(2,1)S(1)}, bf16[32,8192]{1,0:T(8,128)(2,1)S(1)}, u32[]{:S(2)}, u32[]{:S(2)}) collective-permute-start(bf16[32,8192]{1,0:T(8,128)(2,1)S(1)} %get-tuple-element.102), channel_id=1, source_target_pairs={{0,6},{1,7},{2,0},{3,1},{4,2},{5,3},{6,4},{7,5},{8,14},{9,15},{10,... | collective-permute-start | bytes 1572872 | tf_op jit(solution)/shard_map/ppermute | solution.py:26
  99.7 7.5 %collective-permute-start.23 = (bf16[64,1024]{1,0:T(8,128)(2,1)S(1)}, bf16[64,1024]{1,0:T(8,128)(2,1)S(1)}, u32[]{:S(2)}, u32[]{:S(2)}) collective-permute-start(bf16[64,1024]{1,0:T(8,128)(2,1)S(1)} %get-tuple-element.128), channel_id=1, source_target_pairs={{0,48},{8,56},{16,0},{24,8},{32,16},{40,24},{48,32},{56,40},{64,11... | collective-permute-start | bytes 393224 | tf_op jit(solution)/shard_map/ppermute | solution.py:38
  107.4 11.4 %collective-permute-start.26 = (bf16[128,1024]{1,0:T(8,128)(2,1)S(1)}, bf16[128,1024]{1,0:T(8,128)(2,1)S(1)}, u32[]{:S(2)}, u32[]{:S(2)}) collective-permute-start(bf16[128,1024]{1,0:T(8,128)(2,1)S(1)} %get-tuple-element.114), channel_id=1, source_target_pairs={{0,16},{8,24},{16,32},{24,40},{32,48},{40,56},{48,0},{56,8},{64,80... | collective-permute-start | bytes 786440 | tf_op jit(solution)/shard_map/ppermute | solution.py:38
  107.5 11.3 %collective-permute-start.27 = (bf16[128,1024]{1,0:T(8,128)(2,1)S(1)}, bf16[128,1024]{1,0:T(8,128)(2,1)S(1)}, u32[]{:S(2)}, u32[]{:S(2)}) collective-permute-start(bf16[128,1024]{1,0:T(8,128)(2,1)S(1)} %get-tuple-element.115), channel_id=1, source_target_pairs={{0,48},{8,56},{16,0},{24,8},{32,16},{40,24},{48,32},{56,40},{64,11... | collective-permute-start | bytes 786440 | tf_op jit(solution)/shard_map/ppermute | solution.py:38
  (11 other events, 105.0 us)

commit v3 on v2

--- a/solution.py
+++ b/solution.py
@@ -365,7 +365,7 @@
         pass_kernel, v(sum_before, sum_after, sum_low, sum_high), [((rows, 2 * feats), BF)] * 2
     )
     mixed, input_grad = call(
-        rows_kernel, v(tokens, cotangent, sum_own, to_y(sum_after, 1), to_y(sum_before, -1)), [((1, rows, feats), BF)] * 2
+        rows_kernel, v(tokens, cotangent, sum_own, to_y(sum_after, 1), to_y(then(sum_before, (low, high)), -1)), [((1, rows, feats), BF)] * 2
     )
     return (mixed, input_grad, up_grad, down_grad)
 

time: 120 us -> 118 us (0.983)
  waiting for transfers between devices: 54.5 us -> 50.6 us
  starting transfers between devices: 40.5 us -> 42.1 us
    ppermute x6, waiting for transfers between devices: 24.9 us -> 21 us  [to_z(): lax.ppermute(v, 'dp', [(i, i // NZ * NZ + (i % NZ + k) % NZ) for i in ran...]
    ppermute x6, starting transfers between devices: 11.6 us -> 15 us  [to_z(): lax.ppermute(v, 'dp', [(i, i // NZ * NZ + (i % NZ + k) % NZ) for i in ran...]
    ppermute x11, starting transfers between devices: 19.2 us -> 17.5 us  [to_y(): return lax.ppermute(v, 'block', [(i, (i + 2 * k) % 8) for i in range(8)])]
  transfers between devices with their start and end apart: 28 -> 28, of which waited for: 14 -> 14; matrix products, arithmetic and copies ran while one was open for 0% -> 0% of each run, Pallas kernels for 15% -> 16%
where the time goes in v3:
time: 118 us
  waiting for transfers between devices  50.6 us (43%)
  starting transfers between devices  42.1 us (36%)
  Pallas kernels  22.7 us (19%)
  other arithmetic  1.23 us (1%)
    pallas_call x11, Pallas kernels, call(): pl.pallas_call(kernel, out_shape=[jax.ShapeDtypeStruct(shape, kind) for s...  22.7 us
    ppermute x6, waiting for transfers between devices, to_z(): lax.ppermute(v, 'dp', [(i, i // NZ * NZ + (i % NZ + k) % NZ) for i in ran...  21 us
    ppermute x11, starting transfers between devices, to_y(): return lax.ppermute(v, 'block', [(i, (i + 2 * k) % 8) for i in range(8)])  17.5 us
    ppermute x7, waiting for transfers between devices, to_x(): lax.ppermute(v, 'dp', [(i, (i // NZ + k) % NX * NZ + i % NZ) for i in ran...  16.3 us
    ppermute x6, starting transfers between devices, to_z(): lax.ppermute(v, 'dp', [(i, i // NZ * NZ + (i % NZ + k) % NZ) for i in ran...  15 us
    ppermute x11, waiting for transfers between devices, to_y(): return lax.ppermute(v, 'block', [(i, (i + 2 * k) % 8) for i in range(8)])  11.9 us
    ppermute x7, starting transfers between devices, to_x(): lax.ppermute(v, 'dp', [(i, (i // NZ + k) % NX * NZ + i % NZ) for i in ran...  8.5 us
  transfers between devices with their start and end apart: 28, of which 14 were waited for; matrix products, arithmetic and copies ran while one was open for 0% of the time, Pallas kernels for 16%

profile of v3, /device:TPU:6, one launch (start us, length us, event | category | flops | bytes accessed | tf_op | source)
XLA Modules:
  0.0 118.1 jit_solution(16975649930976060438)
XLA Ops:
  3.4 2.9 %collective-permute-start.4 = (bf16[64,4096]{1,0:T(8,128)(2,1)S(1)}, bf16[64,4096]{1,0:T(8,128)(2,1)S(1)}, u32[]{:S(2)}, u32[]{:S(2)}) collective-permute-start(bf16[64,4096]{1,0:T(8,128)(2,1)S(1)} %pad_maximum_fusion.2), channel_id=1, source_target_pairs={{0,4},{1,5},{2,6},{3,7},{4,0},{5,1},{6,2},{7,3},{8,12},{9,13},{10,... | collective-permute-start | bytes 1572872 | tf_op jit(solution)/shard_map/ppermute | solution.py:26
  7.6 2.5 %shard_map.102 = (bf16[32,2048]{1,0:T(8,128)(2,1)}, bf16[32,2048]{1,0:T(8,128)(2,1)}, bf16[32,2048]{1,0:T(8,128)(2,1)}) custom-call(bf16[1,32,4096]{2,1,0:T(8,128)(2,1)} %x.1, bf16[1,32,4096]{2,1,0:T(8,128)(2,1)} %dy.1, s32[32]{0:T(128)} %refs_6_.1), custom_call_target="tpu_custom_call" | custom-call | flops 1 | bytes 1 | tf_op jit(solution)/shard_map/pallas_call | solution.py:48
  10.6 2.4 %collective-permute-start.1 = (bf16[32,2048]{1,0:T(8,128)(2,1)}, bf16[32,2048]{1,0:T(8,128)(2,1)S(1)}, u32[]{:S(2)}, u32[]{:S(2)}) collective-permute-start(bf16[32,2048]{1,0:T(8,128)(2,1)} %get-tuple-element.63), channel_id=1, source_target_pairs={{0,128},{8,136},{16,144},{24,152},{32,160},{40,168},{48,176},{56,1... | collective-permute-start | bytes 393224 | tf_op jit(solution)/shard_map/ppermute | solution.py:34
  13.1 3.1 %collective-permute-done = bf16[32,2048]{1,0:T(8,128)(2,1)S(1)} collective-permute-done((bf16[32,2048]{1,0:T(8,128)(2,1)}, bf16[32,2048]{1,0:T(8,128)(2,1)S(1)}, u32[]{:S(2)}, u32[]{:S(2)}) %collective-permute-start) | collective-permute-done | bytes 131104 | tf_op jit(solution)/shard_map/ppermute | solution.py:34
  17.4 5.1 %collective-permute-done.2 = bf16[32,2048]{1,0:T(8,128)(2,1)S(1)} collective-permute-done((bf16[32,2048]{1,0:T(8,128)(2,1)}, bf16[32,2048]{1,0:T(8,128)(2,1)S(1)}, u32[]{:S(2)}, u32[]{:S(2)}) %collective-permute-start.2) | collective-permute-done | bytes 131104 | tf_op jit(solution)/shard_map/ppermute | solution.py:34
  22.6 6.6 %collective-permute-done.4 = bf16[64,4096]{1,0:T(8,128)(2,1)S(1)} collective-permute-done((bf16[64,4096]{1,0:T(8,128)(2,1)S(1)}, bf16[64,4096]{1,0:T(8,128)(2,1)S(1)}, u32[]{:S(2)}, u32[]{:S(2)}) %collective-permute-start.4) | collective-permute-done | bytes 524320 | tf_op jit(solution)/shard_map/ppermute | solution.py:26
  31.6 2.0 %collective-permute-start.9 = (bf16[32,6144]{1,0:T(8,128)(2,1)S(1)}, bf16[32,6144]{1,0:T(8,128)(2,1)S(1)}, u32[]{:S(2)}, u32[]{:S(2)}) collective-permute-start(bf16[32,6144]{1,0:T(8,128)(2,1)S(1)} %get-tuple-element.133), channel_id=1, source_target_pairs={{0,6},{1,7},{2,0},{3,1},{4,2},{5,3},{6,4},{7,5},{8,14},{9,15},{10,... | collective-permute-start | bytes 1179656 | tf_op jit(solution)/shard_map/ppermute | solution.py:26
  33.6 4.3 %shard_map.103 = (bf16[256,512]{1,0:T(8,128)(2,1)S(1)}, f32[256,512]{1,0:T(8,128)S(1)}) custom-call(bf16[128,4096]{1,0:T(8,128)(2,1)S(1)} %pad_maximum_fusion.1.mine.refs_0_, bf16[128,4096]{1,0:T(8,128)(2,1)S(1)} %collective-permute-done.6.other.refs_1_, bf16[1,4096,512]{2,1,0:T(8,128)(2,1)} %w1.3, s32[32]{0:T(128)S(1)} %copy-done.4, s32[8,32]{1,0:T(8,128)S(1)} %bitcast.5), custom_call_target="tpu_custom_call" | custom-call | flops 1 | bytes 1 | tf_op jit(solution)/shard_map/pallas_call | solution.py:48
  37.9 2.9 %shard_map.104.out = bf16[256,4096]{1,0:T(8,128)(2,1)S(1)} custom-call(bf16[256,512]{1,0:T(8,128)(2,1)S(1)} %get-tuple-element.75.hidden, bf16[1,512,4096]{2,1,0:T(8,128)(2,1)S(1)} %copy-done.1, s32[32]{0:T(128)S(1)} %copy-done.4), custom_call_target="tpu_custom_call" | custom-call | flops 1 | bytes 1 | tf_op jit(solution)/shard_map/pallas_call | solution.py:48
  42.6 2.7 %shard_map.105.both.refs_7_ = bf16[256,1024]{1,0:T(8,128)(2,1)S(1)} custom-call(bf16[128,4096]{1,0:T(8,128)(2,1)S(1)} %pad_maximum_fusion.mine.refs_2_, bf16[128,4096]{1,0:T(8,128)(2,1)S(1)} %collective-permute-done.7.other.refs_3_, bf16[1,512,4096]{2,1,0:T(8,128)(2,1)S(1)} %copy-done.1, s32[32]{0:T(128)S(1)} %copy-done.4, ...), custom_call_target="tpu_custom_call" | custom-call | flops 1 | bytes 1 | tf_op jit(solution)/shard_map/pallas_call | solution.py:48
  48.6 2.9 %shard_map.106 = (bf16[128,8192]{1,0:T(8,128)(2,1)S(1)}, bf16[128,8192]{1,0:T(8,128)(2,1)S(1)}) custom-call(bf16[256,1024]{1,0:T(8,128)(2,1)S(1)} %shard_map.105.both.refs_7_, bf16[1,4096,512]{2,1,0:T(8,128)(2,1)S(1)} %copy-done, bf16[256,4096]{1,0:T(8,128)(2,1)S(1)} %shard_map.104.out, s32[32]{0:T(128)S(1)} %copy-done.4), custom_call_target="tpu_custom_call" | custom-call | flops 1 | bytes 1 | tf_op jit(solution)/shard_map/pallas_call | solution.py:48
  51.6 2.3 %collective-permute-start.13 = (bf16[16,6144]{1,0:T(8,128)(2,1)S(1)}, bf16[16,6144]{1,0:T(8,128)(2,1)S(1)}, u32[]{:S(2)}, u32[]{:S(2)}) collective-permute-start(bf16[16,6144]{1,0:T(8,128)(2,1)S(1)} %slice.57), channel_id=1, source_target_pairs={{0,6},{1,7},{2,0},{3,1},{4,2},{5,3},{6,4},{7,5},{8,14},{9,15},{10,... | collective-permute-start | bytes 589832 | tf_op jit(solution)/shard_map/ppermute | solution.py:26
  54.5 2.8 %collective-permute-done.13 = bf16[16,6144]{1,0:T(8,128)(2,1)S(1)} collective-permute-done((bf16[16,6144]{1,0:T(8,128)(2,1)S(1)}, bf16[16,6144]{1,0:T(8,128)(2,1)S(1)}, u32[]{:S(2)}, u32[]{:S(2)}) %collective-permute-start.13) | collective-permute-done | bytes 196640 | tf_op jit(solution)/shard_map/ppermute | solution.py:26
  60.8 1.9 %collective-permute-start.15 = (bf16[128,1024]{1,0:T(8,128)(2,1)S(1)}, bf16[128,1024]{1,0:T(8,128)(2,1)S(1)}, u32[]{:S(2)}, u32[]{:S(2)}) collective-permute-start(bf16[128,1024]{1,0:T(8,128)(2,1)S(1)} %slice.59), channel_id=1, source_target_pairs={{0,192},{8,200},{16,208},{24,216},{32,224},{40,232},{48,240},{56,2... | collective-permute-start | bytes 786440 | tf_op jit(solution)/shard_map/ppermute | solution.py:34
  64.6 4.2 %collective-permute-done.14.refs_9_ = bf16[128,1024]{1,0:T(8,128)(2,1)S(1)} collective-permute-done((bf16[128,1024]{1,0:T(8,128)(2,1)S(1)}, bf16[128,1024]{1,0:T(8,128)(2,1)S(1)}, u32[]{:S(2)}, u32[]{:S(2)}) %collective-permute-start.14) | collective-permute-done | bytes 262176 | tf_op jit(solution)/shard_map/ppermute | solution.py:34
  70.9 2.5 %collective-permute-start.19 = (bf16[16,8192]{1,0:T(8,128)(2,1)S(1)}, bf16[16,8192]{1,0:T(8,128)(2,1)S(1)}, u32[]{:S(2)}, u32[]{:S(2)}) collective-permute-start(bf16[16,8192]{1,0:T(8,128)(2,1)S(1)} %get-tuple-element.120), channel_id=1, source_target_pairs={{0,6},{1,7},{2,0},{3,1},{4,2},{5,3},{6,4},{7,5},{8,14},{9,15},{10,... | collective-permute-start | bytes 786440 | tf_op jit(solution)/shard_map/ppermute | solution.py:26
  73.5 4.1 %shard_map.108 = (bf16[128,1024]{1,0:T(8,128)(2,1)S(1)}, bf16[256,1024]{1,0:T(8,128)(2,1)S(1)}, bf16[256,1024]{1,0:T(8,128)(2,1)S(1)}, f32[2,128,1024]{2,1,0:T(8,128)S(1)}, f32[128,1024]{1,0:T(8,128)S(1)}) custom-call(bf16[128,4096]{1,0:T(8,128)(2,1)S(1)} %pad_maximum_fusion.1.mine.refs_0_, bf16[128,4096]{1,0:T(8,128)(2,1)S(1)} %collective-permute-done.6.other.refs_1_, ...), custom_call_target="tpu_custom_call" | custom-call | flops 1 | bytes 1 | tf_op jit(solution)/shard_map/pallas_call | solution.py:48
  77.6 2.0 %collective-permute-start.23 = (bf16[256,1024]{1,0:T(8,128)(2,1)S(1)}, bf16[256,1024]{1,0:T(8,128)(2,1)S(1)}, u32[]{:S(2)}, u32[]{:S(2)}) collective-permute-start(bf16[256,1024]{1,0:T(8,128)(2,1)S(1)} %get-tuple-element.105), channel_id=1, source_target_pairs={{0,8},{8,16},{16,24},{24,32},{32,40},{40,48},{48,56},{56,0},{64,72... | collective-permute-start | bytes 1572872 | tf_op jit(solution)/shard_map/ppermute | solution.py:38
  79.6 4.2 %collective-permute-start.24 = (bf16[256,1024]{1,0:T(8,128)(2,1)S(1)}, bf16[256,1024]{1,0:T(8,128)(2,1)S(1)}, u32[]{:S(2)}, u32[]{:S(2)}) collective-permute-start(bf16[256,1024]{1,0:T(8,128)(2,1)S(1)} %get-tuple-element.106), channel_id=1, source_target_pairs={{0,56},{8,0},{16,8},{24,16},{32,24},{40,32},{48,40},{56,48},{64,12... | collective-permute-start | bytes 1572872 | tf_op jit(solution)/shard_map/ppermute | solution.py:38
  84.0 4.1 %collective-permute-start.22 = (bf16[64,1024]{1,0:T(8,128)(2,1)S(1)}, bf16[64,1024]{1,0:T(8,128)(2,1)S(1)}, u32[]{:S(2)}, u32[]{:S(2)}) collective-permute-start(bf16[64,1024]{1,0:T(8,128)(2,1)S(1)} %get-tuple-element.130), channel_id=1, source_target_pairs={{0,48},{8,56},{16,0},{24,8},{32,16},{40,24},{48,32},{56,40},{64,11... | collective-permute-start | bytes 393224 | tf_op jit(solution)/shard_map/ppermute | solution.py:38
  88.3 11.4 %collective-permute-done.21.low = bf16[64,1024]{1,0:T(8,128)(2,1)S(1)} collective-permute-done((bf16[64,1024]{1,0:T(8,128)(2,1)S(1)}, bf16[64,1024]{1,0:T(8,128)(2,1)S(1)}, u32[]{:S(2)}, u32[]{:S(2)}) %collective-permute-start.21) | collective-permute-done | bytes 131104 | tf_op jit(solution)/shard_map/ppermute | solution.py:38
  101.4 4.5 %collective-permute-start.26 = (bf16[128,1024]{1,0:T(8,128)(2,1)S(1)}, bf16[128,1024]{1,0:T(8,128)(2,1)S(1)}, u32[]{:S(2)}, u32[]{:S(2)}) collective-permute-start(bf16[128,1024]{1,0:T(8,128)(2,1)S(1)} %get-tuple-element.116), channel_id=1, source_target_pairs={{0,16},{8,24},{16,32},{24,40},{32,48},{40,56},{48,0},{56,8},{64,80... | collective-permute-start | bytes 786440 | tf_op jit(solution)/shard_map/ppermute | solution.py:38
  105.9 7.4 %collective-permute-done.26.up_far = bf16[128,1024]{1,0:T(8,128)(2,1)S(1)} collective-permute-done((bf16[128,1024]{1,0:T(8,128)(2,1)S(1)}, bf16[128,1024]{1,0:T(8,128)(2,1)S(1)}, u32[]{:S(2)}, u32[]{:S(2)}) %collective-permute-start.26) | collective-permute-done | bytes 262176 | tf_op jit(solution)/shard_map/ppermute | solution.py:38
  113.3 2.2 %collective-permute-done.27.down_far = bf16[128,1024]{1,0:T(8,128)(2,1)S(1)} collective-permute-done((bf16[128,1024]{1,0:T(8,128)(2,1)S(1)}, bf16[128,1024]{1,0:T(8,128)(2,1)S(1)}, u32[]{:S(2)}, u32[]{:S(2)}) %collective-permute-start.27) | collective-permute-done | bytes 262176 | tf_op jit(solution)/shard_map/ppermute | solution.py:38
  (75 shorter events, 26.1 us)
Async XLA Ops:
  1.7 20.9 %collective-permute-start.3 = (bf16[64,4096]{1,0:T(8,128)(2,1)S(1)}, bf16[64,4096]{1,0:T(8,128)(2,1)S(1)}, u32[]{:S(2)}, u32[]{:S(2)}) collective-permute-start(bf16[64,4096]{1,0:T(8,128)(2,1)S(1)} %pad_maximum_fusion.2), channel_id=1, source_target_pairs={{0,2},{1,3},{2,4},{3,5},{4,6},{5,7},{6,0},{7,1},{8,10},{9,11},{10,... | collective-permute-start | bytes 1572872 | tf_op jit(solution)/shard_map/ppermute | solution.py:26
  3.4 25.8 %collective-permute-start.4 = (bf16[64,4096]{1,0:T(8,128)(2,1)S(1)}, bf16[64,4096]{1,0:T(8,128)(2,1)S(1)}, u32[]{:S(2)}, u32[]{:S(2)}) collective-permute-start(bf16[64,4096]{1,0:T(8,128)(2,1)S(1)} %pad_maximum_fusion.2), channel_id=1, source_target_pairs={{0,4},{1,5},{2,6},{3,7},{4,0},{5,1},{6,2},{7,3},{8,12},{9,13},{10,... | collective-permute-start | bytes 1572872 | tf_op jit(solution)/shard_map/ppermute | solution.py:26
  6.3 22.9 %collective-permute-start.5 = (bf16[64,4096]{1,0:T(8,128)(2,1)S(1)}, bf16[64,4096]{1,0:T(8,128)(2,1)S(1)}, u32[]{:S(2)}, u32[]{:S(2)}) collective-permute-start(bf16[64,4096]{1,0:T(8,128)(2,1)S(1)} %pad_maximum_fusion.2), channel_id=1, source_target_pairs={{0,6},{1,7},{2,0},{3,1},{4,2},{5,3},{6,4},{7,5},{8,14},{9,15},{10,... | collective-permute-start | bytes 1572872 | tf_op jit(solution)/shard_map/ppermute | solution.py:26
  10.6 6.8 %collective-permute-start.1 = (bf16[32,2048]{1,0:T(8,128)(2,1)}, bf16[32,2048]{1,0:T(8,128)(2,1)S(1)}, u32[]{:S(2)}, u32[]{:S(2)}) collective-permute-start(bf16[32,2048]{1,0:T(8,128)(2,1)} %get-tuple-element.63), channel_id=1, source_target_pairs={{0,128},{8,136},{16,144},{24,152},{32,160},{40,168},{48,176},{56,1... | collective-permute-start | bytes 393224 | tf_op jit(solution)/shard_map/ppermute | solution.py:34
  16.2 6.4 %collective-permute-start.2 = (bf16[32,2048]{1,0:T(8,128)(2,1)}, bf16[32,2048]{1,0:T(8,128)(2,1)S(1)}, u32[]{:S(2)}, u32[]{:S(2)}) collective-permute-start(bf16[32,2048]{1,0:T(8,128)(2,1)} %get-tuple-element.64), channel_id=1, source_target_pairs={{0,192},{8,200},{16,208},{24,216},{32,224},{40,232},{48,240},{56,2... | collective-permute-start | bytes 393224 | tf_op jit(solution)/shard_map/ppermute | solution.py:34
  29.6 13.0 %collective-permute-start.7 = (bf16[128,4096]{1,0:T(8,128)(2,1)S(1)}, bf16[128,4096]{1,0:T(8,128)(2,1)S(1)}, u32[]{:S(2)}, u32[]{:S(2)}) collective-permute-start(bf16[128,4096]{1,0:T(8,128)(2,1)S(1)} %pad_maximum_fusion.mine.refs_2_), channel_id=1, source_target_pairs={{0,1},{1,0},{2,3},{3,2},{4,5},{5,4},{6,7},{7,6},{8,9},{9,8},{10,11... | collective-permute-start | bytes 3145736 | tf_op jit(solution)/shard_map/ppermute | solution.py:30
  30.3 12.3 %collective-permute-start.8 = (bf16[32,6144]{1,0:T(8,128)(2,1)S(1)}, bf16[32,6144]{1,0:T(8,128)(2,1)S(1)}, u32[]{:S(2)}, u32[]{:S(2)}) collective-permute-start(bf16[32,6144]{1,0:T(8,128)(2,1)S(1)} %get-tuple-element.133), channel_id=1, source_target_pairs={{0,2},{1,3},{2,4},{3,5},{4,6},{5,7},{6,0},{7,1},{8,10},{9,11},{10,... | collective-permute-start | bytes 1179656 | tf_op jit(solution)/shard_map/ppermute | solution.py:26
  31.6 11.0 %collective-permute-start.9 = (bf16[32,6144]{1,0:T(8,128)(2,1)S(1)}, bf16[32,6144]{1,0:T(8,128)(2,1)S(1)}, u32[]{:S(2)}, u32[]{:S(2)}) collective-permute-start(bf16[32,6144]{1,0:T(8,128)(2,1)S(1)} %get-tuple-element.133), channel_id=1, source_target_pairs={{0,6},{1,7},{2,0},{3,1},{4,2},{5,3},{6,4},{7,5},{8,14},{9,15},{10,... | collective-permute-start | bytes 1179656 | tf_op jit(solution)/shard_map/ppermute | solution.py:26
  45.4 13.1 %collective-permute-start.10 = (bf16[256,1024]{1,0:T(8,128)(2,1)S(1)}, bf16[256,1024]{1,0:T(8,128)(2,1)S(1)}, u32[]{:S(2)}, u32[]{:S(2)}) collective-permute-start(bf16[256,1024]{1,0:T(8,128)(2,1)S(1)} %shard_map.105.both.refs_7_), channel_id=1, source_target_pairs={{0,64},{8,72},{16,80},{24,88},{32,96},{40,104},{48,112},{56,120},{... | collective-permute-start | bytes 1572872 | tf_op jit(solution)/shard_map/ppermute | solution.py:34
  45.9 14.0 %collective-permute-start.11 = (bf16[256,1024]{1,0:T(8,128)(2,1)S(1)}, bf16[256,1024]{1,0:T(8,128)(2,1)S(1)}, u32[]{:S(2)}, u32[]{:S(2)}) collective-permute-start(bf16[256,1024]{1,0:T(8,128)(2,1)S(1)} %shard_map.105.both.refs_7_), channel_id=1, source_target_pairs={{0,192},{8,200},{16,208},{24,216},{32,224},{40,232},{48,240},{56,2... | collective-permute-start | bytes 1572872 | tf_op jit(solution)/shard_map/ppermute | solution.py:34
  47.5 7.0 %collective-permute-start.12 = (bf16[16,6144]{1,0:T(8,128)(2,1)S(1)}, bf16[16,6144]{1,0:T(8,128)(2,1)S(1)}, u32[]{:S(2)}, u32[]{:S(2)}) collective-permute-start(bf16[16,6144]{1,0:T(8,128)(2,1)S(1)} %slice.56), channel_id=1, source_target_pairs={{0,2},{1,3},{2,4},{3,5},{4,6},{5,7},{6,0},{7,1},{8,10},{9,11},{10,... | collective-permute-start | bytes 589832 | tf_op jit(solution)/shard_map/ppermute | solution.py:26
  60.0 10.2 %collective-permute-start.16 = (bf16[128,6144]{1,0:T(8,128)(2,1)S(1)}, bf16[128,6144]{1,0:T(8,128)(2,1)S(1)}, u32[]{:S(2)}, u32[]{:S(2)}) collective-permute-start(bf16[128,6144]{1,0:T(8,128)(2,1)S(1)} %constant_dynamic-update-slice_fusion.3.refs_4_), channel_id=1, source_target_pairs={{0,1},{1,0},{2,3},{3,2},{4,5},{5,4},{6,7},{7,6},{8,9},{9,8},{10,11... | collective-permute-start | bytes 4718600 | tf_op jit(solution)/shard_map/ppermute | solution.py:30
  60.5 8.3 %collective-permute-start.14 = (bf16[128,1024]{1,0:T(8,128)(2,1)S(1)}, bf16[128,1024]{1,0:T(8,128)(2,1)S(1)}, u32[]{:S(2)}, u32[]{:S(2)}) collective-permute-start(bf16[128,1024]{1,0:T(8,128)(2,1)S(1)} %slice.58), channel_id=1, source_target_pairs={{0,64},{8,72},{16,80},{24,88},{32,96},{40,104},{48,112},{56,120},{... | collective-permute-start | bytes 786440 | tf_op jit(solution)/shard_map/ppermute | solution.py:34
  60.8 9.3 %collective-permute-start.15 = (bf16[128,1024]{1,0:T(8,128)(2,1)S(1)}, bf16[128,1024]{1,0:T(8,128)(2,1)S(1)}, u32[]{:S(2)}, u32[]{:S(2)}) collective-permute-start(bf16[128,1024]{1,0:T(8,128)(2,1)S(1)} %slice.59), channel_id=1, source_target_pairs={{0,192},{8,200},{16,208},{24,216},{32,224},{40,232},{48,240},{56,2... | collective-permute-start | bytes 786440 | tf_op jit(solution)/shard_map/ppermute | solution.py:34
  70.1 13.7 %collective-permute-start.18 = (bf16[16,8192]{1,0:T(8,128)(2,1)S(1)}, bf16[16,8192]{1,0:T(8,128)(2,1)S(1)}, u32[]{:S(2)}, u32[]{:S(2)}) collective-permute-start(bf16[16,8192]{1,0:T(8,128)(2,1)S(1)} %get-tuple-element.121), channel_id=1, source_target_pairs={{0,2},{1,3},{2,4},{3,5},{4,6},{5,7},{6,0},{7,1},{8,10},{9,11},{10,... | collective-permute-start | bytes 786440 | tf_op jit(solution)/shard_map/ppermute | solution.py:26
  70.9 12.9 %collective-permute-start.19 = (bf16[16,8192]{1,0:T(8,128)(2,1)S(1)}, bf16[16,8192]{1,0:T(8,128)(2,1)S(1)}, u32[]{:S(2)}, u32[]{:S(2)}) collective-permute-start(bf16[16,8192]{1,0:T(8,128)(2,1)S(1)} %get-tuple-element.120), channel_id=1, source_target_pairs={{0,6},{1,7},{2,0},{3,1},{4,2},{5,3},{6,4},{7,5},{8,14},{9,15},{10,... | collective-permute-start | bytes 786440 | tf_op jit(solution)/shard_map/ppermute | solution.py:26
  77.6 22.1 %collective-permute-start.23 = (bf16[256,1024]{1,0:T(8,128)(2,1)S(1)}, bf16[256,1024]{1,0:T(8,128)(2,1)S(1)}, u32[]{:S(2)}, u32[]{:S(2)}) collective-permute-start(bf16[256,1024]{1,0:T(8,128)(2,1)S(1)} %get-tuple-element.105), channel_id=1, source_target_pairs={{0,8},{8,16},{16,24},{24,32},{32,40},{40,48},{48,56},{56,0},{64,72... | collective-permute-start | bytes 1572872 | tf_op jit(solution)/shard_map/ppermute | solution.py:38
  79.6 20.1 %collective-permute-start.24 = (bf16[256,1024]{1,0:T(8,128)(2,1)S(1)}, bf16[256,1024]{1,0:T(8,128)(2,1)S(1)}, u32[]{:S(2)}, u32[]{:S(2)}) collective-permute-start(bf16[256,1024]{1,0:T(8,128)(2,1)S(1)} %get-tuple-element.106), channel_id=1, source_target_pairs={{0,56},{8,0},{16,8},{24,16},{32,24},{40,32},{48,40},{56,48},{64,12... | collective-permute-start | bytes 1572872 | tf_op jit(solution)/shard_map/ppermute | solution.py:38
  83.9 15.8 %collective-permute-start.21 = (bf16[64,1024]{1,0:T(8,128)(2,1)S(1)}, bf16[64,1024]{1,0:T(8,128)(2,1)S(1)}, u32[]{:S(2)}, u32[]{:S(2)}) collective-permute-start(bf16[64,1024]{1,0:T(8,128)(2,1)S(1)} %get-tuple-element.131), channel_id=1, source_target_pairs={{0,16},{8,24},{16,32},{24,40},{32,48},{40,56},{48,0},{56,8},{64,80... | collective-permute-start | bytes 393224 | tf_op jit(solution)/shard_map/ppermute | solution.py:38
  84.0 15.8 %collective-permute-start.22 = (bf16[64,1024]{1,0:T(8,128)(2,1)S(1)}, bf16[64,1024]{1,0:T(8,128)(2,1)S(1)}, u32[]{:S(2)}, u32[]{:S(2)}) collective-permute-start(bf16[64,1024]{1,0:T(8,128)(2,1)S(1)} %get-tuple-element.130), channel_id=1, source_target_pairs={{0,48},{8,56},{16,0},{24,8},{32,16},{40,24},{48,32},{56,40},{64,11... | collective-permute-start | bytes 393224 | tf_op jit(solution)/shard_map/ppermute | solution.py:38
  88.2 28.8 %collective-permute-start.20 = (bf16[32,8192]{1,0:T(8,128)(2,1)S(1)}, bf16[32,8192]{1,0:T(8,128)(2,1)S(1)}, u32[]{:S(2)}, u32[]{:S(2)}) collective-permute-start(bf16[32,8192]{1,0:T(8,128)(2,1)S(1)} %get-tuple-element.102), channel_id=1, source_target_pairs={{0,2},{1,3},{2,4},{3,5},{4,6},{5,7},{6,0},{7,1},{8,10},{9,11},{10,... | collective-permute-start | bytes 1572872 | tf_op jit(solution)/shard_map/ppermute | solution.py:26
  99.7 17.3 %collective-permute-start.25 = (bf16[32,8192]{1,0:T(8,128)(2,1)S(1)}, bf16[32,8192]{1,0:T(8,128)(2,1)S(1)}, u32[]{:S(2)}, u32[]{:S(2)}) collective-permute-start(bf16[32,8192]{1,0:T(8,128)(2,1)S(1)} %get-tuple-element.109), channel_id=1, source_target_pairs={{0,6},{1,7},{2,0},{3,1},{4,2},{5,3},{6,4},{7,5},{8,14},{9,15},{10,... | collective-permute-start | bytes 1572872 | tf_op jit(solution)/shard_map/ppermute | solution.py:26
  101.4 11.9 %collective-permute-start.26 = (bf16[128,1024]{1,0:T(8,128)(2,1)S(1)}, bf16[128,1024]{1,0:T(8,128)(2,1)S(1)}, u32[]{:S(2)}, u32[]{:S(2)}) collective-permute-start(bf16[128,1024]{1,0:T(8,128)(2,1)S(1)} %get-tuple-element.116), channel_id=1, source_target_pairs={{0,16},{8,24},{16,32},{24,40},{32,48},{40,56},{48,0},{56,8},{64,80... | collective-permute-start | bytes 786440 | tf_op jit(solution)/shard_map/ppermute | solution.py:38
  105.9 9.6 %collective-permute-start.27 = (bf16[128,1024]{1,0:T(8,128)(2,1)S(1)}, bf16[128,1024]{1,0:T(8,128)(2,1)S(1)}, u32[]{:S(2)}, u32[]{:S(2)}) collective-permute-start(bf16[128,1024]{1,0:T(8,128)(2,1)S(1)} %get-tuple-element.117), channel_id=1, source_target_pairs={{0,48},{8,56},{16,0},{24,8},{32,16},{40,24},{48,32},{56,40},{64,11... | collective-permute-start | bytes 786440 | tf_op jit(solution)/shard_map/ppermute | solution.py:38
  (11 other events, 97.3 us)

commit v4 on v3

--- a/solution.py
+++ b/solution.py
@@ -304,9 +304,6 @@
         [held_down, sems(CHUNKS)],
         24,
     )
-    hidden, slope, other_dy, before, after, out = together(
-        hidden, slope, other_dy, before, after, out
-    )
 
     (both,) = call(
         grad_kernel,
@@ -315,6 +312,8 @@
         [held_down, sems(CHUNKS)],
         24,
     )
+    both, before, after, out = together(both, before, after, out)
+
     left, right = to_x(both, 1), to_x(both, -1)
     half = rows // 2
     far = [to_y(before[:half], 1), to_y(after[half:], -1)]

time: 118 us -> 116 us (0.983)
  waiting for transfers between devices: 50.6 us -> 49.1 us
    ppermute x11, waiting for transfers between devices: 11.9 us -> 9.75 us  [to_y(): return lax.ppermute(v, 'block', [(i, (i + 2 * k) % 8) for i in range(8)])]
  transfers between devices with their start and end apart: 28 -> 28, of which waited for: 14 -> 13; matrix products, arithmetic and copies ran while one was open for 0% -> 0% of each run, Pallas kernels for 16% -> 19%
where the time goes in v4:
time: 116 us
  waiting for transfers between devices  49.1 us (42%)
  starting transfers between devices  41.6 us (36%)
  Pallas kernels  22.7 us (20%)
  other arithmetic  1.23 us (1%)
    pallas_call x11, Pallas kernels, call(): pl.pallas_call(kernel, out_shape=[jax.ShapeDtypeStruct(shape, kind) for s...  22.7 us
    ppermute x6, waiting for transfers between devices, to_z(): lax.ppermute(v, 'dp', [(i, i // NZ * NZ + (i % NZ + k) % NZ) for i in ran...  21 us
    ppermute x11, starting transfers between devices, to_y(): return lax.ppermute(v, 'block', [(i, (i + 2 * k) % 8) for i in range(8)])  17 us
    ppermute x7, waiting for transfers between devices, to_x(): lax.ppermute(v, 'dp', [(i, (i // NZ + k) % NX * NZ + i % NZ) for i in ran...  16.9 us
    ppermute x6, starting transfers between devices, to_z(): lax.ppermute(v, 'dp', [(i, i // NZ * NZ + (i % NZ + k) % NZ) for i in ran...  15 us
    ppermute x11, waiting for transfers between devices, to_y(): return lax.ppermute(v, 'block', [(i, (i + 2 * k) % 8) for i in range(8)])  9.75 us
    ppermute x7, starting transfers between devices, to_x(): lax.ppermute(v, 'dp', [(i, (i // NZ + k) % NX * NZ + i % NZ) for i in ran...  8.5 us
  transfers between devices with their start and end apart: 28, of which 13 were waited for; matrix products, arithmetic and copies ran while one was open for 0% of the time, Pallas kernels for 19%

profile of v4, /device:TPU:6, one launch (start us, length us, event | category | flops | bytes accessed | tf_op | source)
XLA Modules:
  0.0 116.1 jit_solution(2275823596678703242)
XLA Ops:
  3.4 2.9 %collective-permute-start.4 = (bf16[64,4096]{1,0:T(8,128)(2,1)S(1)}, bf16[64,4096]{1,0:T(8,128)(2,1)S(1)}, u32[]{:S(2)}, u32[]{:S(2)}) collective-permute-start(bf16[64,4096]{1,0:T(8,128)(2,1)S(1)} %pad_maximum_fusion.2), channel_id=1, source_target_pairs={{0,4},{1,5},{2,6},{3,7},{4,0},{5,1},{6,2},{7,3},{8,12},{9,13},{10,... | collective-permute-start | bytes 1572872 | tf_op jit(solution)/shard_map/ppermute | solution.py:26
  7.6 2.5 %shard_map.102 = (bf16[32,2048]{1,0:T(8,128)(2,1)}, bf16[32,2048]{1,0:T(8,128)(2,1)}, bf16[32,2048]{1,0:T(8,128)(2,1)}) custom-call(bf16[1,32,4096]{2,1,0:T(8,128)(2,1)} %x.1, bf16[1,32,4096]{2,1,0:T(8,128)(2,1)} %dy.1, s32[32]{0:T(128)} %refs_6_.1), custom_call_target="tpu_custom_call" | custom-call | flops 1 | bytes 1 | tf_op jit(solution)/shard_map/pallas_call | solution.py:48
  10.6 2.4 %collective-permute-start.1 = (bf16[32,2048]{1,0:T(8,128)(2,1)}, bf16[32,2048]{1,0:T(8,128)(2,1)S(1)}, u32[]{:S(2)}, u32[]{:S(2)}) collective-permute-start(bf16[32,2048]{1,0:T(8,128)(2,1)} %get-tuple-element.61), channel_id=1, source_target_pairs={{0,128},{8,136},{16,144},{24,152},{32,160},{40,168},{48,176},{56,1... | collective-permute-start | bytes 393224 | tf_op jit(solution)/shard_map/ppermute | solution.py:34
  13.1 3.1 %collective-permute-done = bf16[32,2048]{1,0:T(8,128)(2,1)S(1)} collective-permute-done((bf16[32,2048]{1,0:T(8,128)(2,1)}, bf16[32,2048]{1,0:T(8,128)(2,1)S(1)}, u32[]{:S(2)}, u32[]{:S(2)}) %collective-permute-start) | collective-permute-done | bytes 131104 | tf_op jit(solution)/shard_map/ppermute | solution.py:34
  17.4 5.1 %collective-permute-done.2 = bf16[32,2048]{1,0:T(8,128)(2,1)S(1)} collective-permute-done((bf16[32,2048]{1,0:T(8,128)(2,1)}, bf16[32,2048]{1,0:T(8,128)(2,1)S(1)}, u32[]{:S(2)}, u32[]{:S(2)}) %collective-permute-start.2) | collective-permute-done | bytes 131104 | tf_op jit(solution)/shard_map/ppermute | solution.py:34
  22.6 6.6 %collective-permute-done.4 = bf16[64,4096]{1,0:T(8,128)(2,1)S(1)} collective-permute-done((bf16[64,4096]{1,0:T(8,128)(2,1)S(1)}, bf16[64,4096]{1,0:T(8,128)(2,1)S(1)}, u32[]{:S(2)}, u32[]{:S(2)}) %collective-permute-start.4) | collective-permute-done | bytes 524320 | tf_op jit(solution)/shard_map/ppermute | solution.py:26
  31.6 2.0 %collective-permute-start.9 = (bf16[32,6144]{1,0:T(8,128)(2,1)S(1)}, bf16[32,6144]{1,0:T(8,128)(2,1)S(1)}, u32[]{:S(2)}, u32[]{:S(2)}) collective-permute-start(bf16[32,6144]{1,0:T(8,128)(2,1)S(1)} %get-tuple-element.129), channel_id=1, source_target_pairs={{0,6},{1,7},{2,0},{3,1},{4,2},{5,3},{6,4},{7,5},{8,14},{9,15},{10,... | collective-permute-start | bytes 1179656 | tf_op jit(solution)/shard_map/ppermute | solution.py:26
  33.6 4.3 %shard_map.103 = (bf16[256,512]{1,0:T(8,128)(2,1)S(1)}, f32[256,512]{1,0:T(8,128)S(1)}) custom-call(bf16[128,4096]{1,0:T(8,128)(2,1)S(1)} %pad_maximum_fusion.1.mine.refs_0_, bf16[128,4096]{1,0:T(8,128)(2,1)S(1)} %collective-permute-done.7.other.refs_1_, bf16[1,4096,512]{2,1,0:T(8,128)(2,1)} %w1.3, s32[32]{0:T(128)S(1)} %copy-done.4, s32[8,32]{1,0:T(8,128)S(1)} %bitcast.5), custom_call_target="tpu_custom_call" | custom-call | flops 1 | bytes 1 | tf_op jit(solution)/shard_map/pallas_call | solution.py:48
  37.9 2.9 %shard_map.105.out = bf16[256,4096]{1,0:T(8,128)(2,1)S(1)} custom-call(bf16[256,512]{1,0:T(8,128)(2,1)S(1)} %get-tuple-element.67.hidden, bf16[1,512,4096]{2,1,0:T(8,128)(2,1)S(1)} %copy-done.1, s32[32]{0:T(128)S(1)} %copy-done.4), custom_call_target="tpu_custom_call" | custom-call | flops 1 | bytes 1 | tf_op jit(solution)/shard_map/pallas_call | solution.py:48
  40.8 2.7 %shard_map.104.both.refs_7_ = bf16[256,1024]{1,0:T(8,128)(2,1)S(1)} custom-call(bf16[128,4096]{1,0:T(8,128)(2,1)S(1)} %pad_maximum_fusion.mine.refs_2_, bf16[128,4096]{1,0:T(8,128)(2,1)S(1)} %collective-permute-done.6.other.refs_3_, bf16[1,512,4096]{2,1,0:T(8,128)(2,1)S(1)} %copy-done.1, s32[32]{0:T(128)S(1)} %copy-done.4, ...), custom_call_target="tpu_custom_call" | custom-call | flops 1 | bytes 1 | tf_op jit(solution)/shard_map/pallas_call | solution.py:48
  45.9 2.9 %shard_map.106 = (bf16[128,8192]{1,0:T(8,128)(2,1)S(1)}, bf16[128,8192]{1,0:T(8,128)(2,1)S(1)}) custom-call(bf16[256,1024]{1,0:T(8,128)(2,1)S(1)} %shard_map.104.both.refs_7_, bf16[1,4096,512]{2,1,0:T(8,128)(2,1)S(1)} %copy-done, bf16[256,4096]{1,0:T(8,128)(2,1)S(1)} %shard_map.105.out, s32[32]{0:T(128)S(1)} %copy-done.4), custom_call_target="tpu_custom_call" | custom-call | flops 1 | bytes 1 | tf_op jit(solution)/shard_map/pallas_call | solution.py:48
  48.8 3.3 %collective-permute-start.13 = (bf16[16,6144]{1,0:T(8,128)(2,1)S(1)}, bf16[16,6144]{1,0:T(8,128)(2,1)S(1)}, u32[]{:S(2)}, u32[]{:S(2)}) collective-permute-start(bf16[16,6144]{1,0:T(8,128)(2,1)S(1)} %slice.57), channel_id=1, source_target_pairs={{0,6},{1,7},{2,0},{3,1},{4,2},{5,3},{6,4},{7,5},{8,14},{9,15},{10,... | collective-permute-start | bytes 589832 | tf_op jit(solution)/shard_map/ppermute | solution.py:26
  52.7 2.5 %collective-permute-done.13 = bf16[16,6144]{1,0:T(8,128)(2,1)S(1)} collective-permute-done((bf16[16,6144]{1,0:T(8,128)(2,1)S(1)}, bf16[16,6144]{1,0:T(8,128)(2,1)S(1)}, u32[]{:S(2)}, u32[]{:S(2)}) %collective-permute-start.13) | collective-permute-done | bytes 196640 | tf_op jit(solution)/shard_map/ppermute | solution.py:26
  59.3 1.9 %collective-permute-start.15 = (bf16[128,1024]{1,0:T(8,128)(2,1)S(1)}, bf16[128,1024]{1,0:T(8,128)(2,1)S(1)}, u32[]{:S(2)}, u32[]{:S(2)}) collective-permute-start(bf16[128,1024]{1,0:T(8,128)(2,1)S(1)} %slice.59), channel_id=1, source_target_pairs={{0,192},{8,200},{16,208},{24,216},{32,224},{40,232},{48,240},{56,2... | collective-permute-start | bytes 786440 | tf_op jit(solution)/shard_map/ppermute | solution.py:34
  63.1 4.2 %collective-permute-done.14.refs_9_ = bf16[128,1024]{1,0:T(8,128)(2,1)S(1)} collective-permute-done((bf16[128,1024]{1,0:T(8,128)(2,1)S(1)}, bf16[128,1024]{1,0:T(8,128)(2,1)S(1)}, u32[]{:S(2)}, u32[]{:S(2)}) %collective-permute-start.14) | collective-permute-done | bytes 262176 | tf_op jit(solution)/shard_map/ppermute | solution.py:34
  69.2 2.8 %collective-permute-start.19 = (bf16[16,8192]{1,0:T(8,128)(2,1)S(1)}, bf16[16,8192]{1,0:T(8,128)(2,1)S(1)}, u32[]{:S(2)}, u32[]{:S(2)}) collective-permute-start(bf16[16,8192]{1,0:T(8,128)(2,1)S(1)} %get-tuple-element.116), channel_id=1, source_target_pairs={{0,6},{1,7},{2,0},{3,1},{4,2},{5,3},{6,4},{7,5},{8,14},{9,15},{10,... | collective-permute-start | bytes 786440 | tf_op jit(solution)/shard_map/ppermute | solution.py:26
  72.0 4.1 %shard_map.108 = (bf16[128,1024]{1,0:T(8,128)(2,1)S(1)}, bf16[256,1024]{1,0:T(8,128)(2,1)S(1)}, bf16[256,1024]{1,0:T(8,128)(2,1)S(1)}, f32[2,128,1024]{2,1,0:T(8,128)S(1)}, f32[128,1024]{1,0:T(8,128)S(1)}) custom-call(bf16[128,4096]{1,0:T(8,128)(2,1)S(1)} %pad_maximum_fusion.1.mine.refs_0_, bf16[128,4096]{1,0:T(8,128)(2,1)S(1)} %collective-permute-done.7.other.refs_1_, ...), custom_call_target="tpu_custom_call" | custom-call | flops 1 | bytes 1 | tf_op jit(solution)/shard_map/pallas_call | solution.py:48
  76.1 2.0 %collective-permute-start.23 = (bf16[256,1024]{1,0:T(8,128)(2,1)S(1)}, bf16[256,1024]{1,0:T(8,128)(2,1)S(1)}, u32[]{:S(2)}, u32[]{:S(2)}) collective-permute-start(bf16[256,1024]{1,0:T(8,128)(2,1)S(1)} %get-tuple-element.101), channel_id=1, source_target_pairs={{0,8},{8,16},{16,24},{24,32},{32,40},{40,48},{48,56},{56,0},{64,72... | collective-permute-start | bytes 1572872 | tf_op jit(solution)/shard_map/ppermute | solution.py:38
  78.1 4.2 %collective-permute-start.24 = (bf16[256,1024]{1,0:T(8,128)(2,1)S(1)}, bf16[256,1024]{1,0:T(8,128)(2,1)S(1)}, u32[]{:S(2)}, u32[]{:S(2)}) collective-permute-start(bf16[256,1024]{1,0:T(8,128)(2,1)S(1)} %get-tuple-element.102), channel_id=1, source_target_pairs={{0,56},{8,0},{16,8},{24,16},{32,24},{40,32},{48,40},{56,48},{64,12... | collective-permute-start | bytes 1572872 | tf_op jit(solution)/shard_map/ppermute | solution.py:38
  82.5 4.1 %collective-permute-start.22 = (bf16[64,1024]{1,0:T(8,128)(2,1)S(1)}, bf16[64,1024]{1,0:T(8,128)(2,1)S(1)}, u32[]{:S(2)}, u32[]{:S(2)}) collective-permute-start(bf16[64,1024]{1,0:T(8,128)(2,1)S(1)} %get-tuple-element.126), channel_id=1, source_target_pairs={{0,48},{8,56},{16,0},{24,8},{32,16},{40,24},{48,32},{56,40},{64,11... | collective-permute-start | bytes 393224 | tf_op jit(solution)/shard_map/ppermute | solution.py:38
  86.8 11.4 %collective-permute-done.21.low = bf16[64,1024]{1,0:T(8,128)(2,1)S(1)} collective-permute-done((bf16[64,1024]{1,0:T(8,128)(2,1)S(1)}, bf16[64,1024]{1,0:T(8,128)(2,1)S(1)}, u32[]{:S(2)}, u32[]{:S(2)}) %collective-permute-start.21) | collective-permute-done | bytes 131104 | tf_op jit(solution)/shard_map/ppermute | solution.py:38
  99.4 4.5 %collective-permute-start.26 = (bf16[128,1024]{1,0:T(8,128)(2,1)S(1)}, bf16[128,1024]{1,0:T(8,128)(2,1)S(1)}, u32[]{:S(2)}, u32[]{:S(2)}) collective-permute-start(bf16[128,1024]{1,0:T(8,128)(2,1)S(1)} %get-tuple-element.112), channel_id=1, source_target_pairs={{0,16},{8,24},{16,32},{24,40},{32,48},{40,56},{48,0},{56,8},{64,80... | collective-permute-start | bytes 786440 | tf_op jit(solution)/shard_map/ppermute | solution.py:38
  103.9 7.4 %collective-permute-done.26.up_far = bf16[128,1024]{1,0:T(8,128)(2,1)S(1)} collective-permute-done((bf16[128,1024]{1,0:T(8,128)(2,1)S(1)}, bf16[128,1024]{1,0:T(8,128)(2,1)S(1)}, u32[]{:S(2)}, u32[]{:S(2)}) %collective-permute-start.26) | collective-permute-done | bytes 262176 | tf_op jit(solution)/shard_map/ppermute | solution.py:38
  111.3 2.2 %collective-permute-done.27.down_far = bf16[128,1024]{1,0:T(8,128)(2,1)S(1)} collective-permute-done((bf16[128,1024]{1,0:T(8,128)(2,1)S(1)}, bf16[128,1024]{1,0:T(8,128)(2,1)S(1)}, u32[]{:S(2)}, u32[]{:S(2)}) %collective-permute-start.27) | collective-permute-done | bytes 262176 | tf_op jit(solution)/shard_map/ppermute | solution.py:38
  (75 shorter events, 23.1 us)
Async XLA Ops:
  1.7 20.9 %collective-permute-start.3 = (bf16[64,4096]{1,0:T(8,128)(2,1)S(1)}, bf16[64,4096]{1,0:T(8,128)(2,1)S(1)}, u32[]{:S(2)}, u32[]{:S(2)}) collective-permute-start(bf16[64,4096]{1,0:T(8,128)(2,1)S(1)} %pad_maximum_fusion.2), channel_id=1, source_target_pairs={{0,2},{1,3},{2,4},{3,5},{4,6},{5,7},{6,0},{7,1},{8,10},{9,11},{10,... | collective-permute-start | bytes 1572872 | tf_op jit(solution)/shard_map/ppermute | solution.py:26
  3.4 25.8 %collective-permute-start.4 = (bf16[64,4096]{1,0:T(8,128)(2,1)S(1)}, bf16[64,4096]{1,0:T(8,128)(2,1)S(1)}, u32[]{:S(2)}, u32[]{:S(2)}) collective-permute-start(bf16[64,4096]{1,0:T(8,128)(2,1)S(1)} %pad_maximum_fusion.2), channel_id=1, source_target_pairs={{0,4},{1,5},{2,6},{3,7},{4,0},{5,1},{6,2},{7,3},{8,12},{9,13},{10,... | collective-permute-start | bytes 1572872 | tf_op jit(solution)/shard_map/ppermute | solution.py:26
  6.3 22.9 %collective-permute-start.5 = (bf16[64,4096]{1,0:T(8,128)(2,1)S(1)}, bf16[64,4096]{1,0:T(8,128)(2,1)S(1)}, u32[]{:S(2)}, u32[]{:S(2)}) collective-permute-start(bf16[64,4096]{1,0:T(8,128)(2,1)S(1)} %pad_maximum_fusion.2), channel_id=1, source_target_pairs={{0,6},{1,7},{2,0},{3,1},{4,2},{5,3},{6,4},{7,5},{8,14},{9,15},{10,... | collective-permute-start | bytes 1572872 | tf_op jit(solution)/shard_map/ppermute | solution.py:26
  10.6 6.8 %collective-permute-start.1 = (bf16[32,2048]{1,0:T(8,128)(2,1)}, bf16[32,2048]{1,0:T(8,128)(2,1)S(1)}, u32[]{:S(2)}, u32[]{:S(2)}) collective-permute-start(bf16[32,2048]{1,0:T(8,128)(2,1)} %get-tuple-element.61), channel_id=1, source_target_pairs={{0,128},{8,136},{16,144},{24,152},{32,160},{40,168},{48,176},{56,1... | collective-permute-start | bytes 393224 | tf_op jit(solution)/shard_map/ppermute | solution.py:34
  29.6 11.2 %collective-permute-start.6 = (bf16[128,4096]{1,0:T(8,128)(2,1)S(1)}, bf16[128,4096]{1,0:T(8,128)(2,1)S(1)}, u32[]{:S(2)}, u32[]{:S(2)}) collective-permute-start(bf16[128,4096]{1,0:T(8,128)(2,1)S(1)} %pad_maximum_fusion.mine.refs_2_), channel_id=1, source_target_pairs={{0,1},{1,0},{2,3},{3,2},{4,5},{5,4},{6,7},{7,6},{8,9},{9,8},{10,11... | collective-permute-start | bytes 3145736 | tf_op jit(solution)/shard_map/ppermute | solution.py:30
  30.3 13.3 %collective-permute-start.8 = (bf16[32,6144]{1,0:T(8,128)(2,1)S(1)}, bf16[32,6144]{1,0:T(8,128)(2,1)S(1)}, u32[]{:S(2)}, u32[]{:S(2)}) collective-permute-start(bf16[32,6144]{1,0:T(8,128)(2,1)S(1)} %get-tuple-element.129), channel_id=1, source_target_pairs={{0,2},{1,3},{2,4},{3,5},{4,6},{5,7},{6,0},{7,1},{8,10},{9,11},{10,... | collective-permute-start | bytes 1179656 | tf_op jit(solution)/shard_map/ppermute | solution.py:26
  31.6 12.0 %collective-permute-start.9 = (bf16[32,6144]{1,0:T(8,128)(2,1)S(1)}, bf16[32,6144]{1,0:T(8,128)(2,1)S(1)}, u32[]{:S(2)}, u32[]{:S(2)}) collective-permute-start(bf16[32,6144]{1,0:T(8,128)(2,1)S(1)} %get-tuple-element.129), channel_id=1, source_target_pairs={{0,6},{1,7},{2,0},{3,1},{4,2},{5,3},{6,4},{7,5},{8,14},{9,15},{10,... | collective-permute-start | bytes 1179656 | tf_op jit(solution)/shard_map/ppermute | solution.py:26
  43.6 13.4 %collective-permute-start.10 = (bf16[256,1024]{1,0:T(8,128)(2,1)S(1)}, bf16[256,1024]{1,0:T(8,128)(2,1)S(1)}, u32[]{:S(2)}, u32[]{:S(2)}) collective-permute-start(bf16[256,1024]{1,0:T(8,128)(2,1)S(1)} %shard_map.104.both.refs_7_), channel_id=1, source_target_pairs={{0,64},{8,72},{16,80},{24,88},{32,96},{40,104},{48,112},{56,120},{... | collective-permute-start | bytes 1572872 | tf_op jit(solution)/shard_map/ppermute | solution.py:34
  44.1 14.3 %collective-permute-start.11 = (bf16[256,1024]{1,0:T(8,128)(2,1)S(1)}, bf16[256,1024]{1,0:T(8,128)(2,1)S(1)}, u32[]{:S(2)}, u32[]{:S(2)}) collective-permute-start(bf16[256,1024]{1,0:T(8,128)(2,1)S(1)} %shard_map.104.both.refs_7_), channel_id=1, source_target_pairs={{0,192},{8,200},{16,208},{24,216},{32,224},{40,232},{48,240},{56,2... | collective-permute-start | bytes 1572872 | tf_op jit(solution)/shard_map/ppermute | solution.py:34
  45.7 7.0 %collective-permute-start.12 = (bf16[16,6144]{1,0:T(8,128)(2,1)S(1)}, bf16[16,6144]{1,0:T(8,128)(2,1)S(1)}, u32[]{:S(2)}, u32[]{:S(2)}) collective-permute-start(bf16[16,6144]{1,0:T(8,128)(2,1)S(1)} %slice.56), channel_id=1, source_target_pairs={{0,2},{1,3},{2,4},{3,5},{4,6},{5,7},{6,0},{7,1},{8,10},{9,11},{10,... | collective-permute-start | bytes 589832 | tf_op jit(solution)/shard_map/ppermute | solution.py:26
  48.8 6.5 %collective-permute-start.13 = (bf16[16,6144]{1,0:T(8,128)(2,1)S(1)}, bf16[16,6144]{1,0:T(8,128)(2,1)S(1)}, u32[]{:S(2)}, u32[]{:S(2)}) collective-permute-start(bf16[16,6144]{1,0:T(8,128)(2,1)S(1)} %slice.57), channel_id=1, source_target_pairs={{0,6},{1,7},{2,0},{3,1},{4,2},{5,3},{6,4},{7,5},{8,14},{9,15},{10,... | collective-permute-start | bytes 589832 | tf_op jit(solution)/shard_map/ppermute | solution.py:26
  58.5 10.2 %collective-permute-start.16 = (bf16[128,6144]{1,0:T(8,128)(2,1)S(1)}, bf16[128,6144]{1,0:T(8,128)(2,1)S(1)}, u32[]{:S(2)}, u32[]{:S(2)}) collective-permute-start(bf16[128,6144]{1,0:T(8,128)(2,1)S(1)} %constant_dynamic-update-slice_fusion.3.refs_4_), channel_id=1, source_target_pairs={{0,1},{1,0},{2,3},{3,2},{4,5},{5,4},{6,7},{7,6},{8,9},{9,8},{10,11... | collective-permute-start | bytes 4718600 | tf_op jit(solution)/shard_map/ppermute | solution.py:30
  59.0 8.3 %collective-permute-start.14 = (bf16[128,1024]{1,0:T(8,128)(2,1)S(1)}, bf16[128,1024]{1,0:T(8,128)(2,1)S(1)}, u32[]{:S(2)}, u32[]{:S(2)}) collective-permute-start(bf16[128,1024]{1,0:T(8,128)(2,1)S(1)} %slice.58), channel_id=1, source_target_pairs={{0,64},{8,72},{16,80},{24,88},{32,96},{40,104},{48,112},{56,120},{... | collective-permute-start | bytes 786440 | tf_op jit(solution)/shard_map/ppermute | solution.py:34
  59.3 9.3 %collective-permute-start.15 = (bf16[128,1024]{1,0:T(8,128)(2,1)S(1)}, bf16[128,1024]{1,0:T(8,128)(2,1)S(1)}, u32[]{:S(2)}, u32[]{:S(2)}) collective-permute-start(bf16[128,1024]{1,0:T(8,128)(2,1)S(1)} %slice.59), channel_id=1, source_target_pairs={{0,192},{8,200},{16,208},{24,216},{32,224},{40,232},{48,240},{56,2... | collective-permute-start | bytes 786440 | tf_op jit(solution)/shard_map/ppermute | solution.py:34
  68.7 13.7 %collective-permute-start.18 = (bf16[16,8192]{1,0:T(8,128)(2,1)S(1)}, bf16[16,8192]{1,0:T(8,128)(2,1)S(1)}, u32[]{:S(2)}, u32[]{:S(2)}) collective-permute-start(bf16[16,8192]{1,0:T(8,128)(2,1)S(1)} %get-tuple-element.117), channel_id=1, source_target_pairs={{0,2},{1,3},{2,4},{3,5},{4,6},{5,7},{6,0},{7,1},{8,10},{9,11},{10,... | collective-permute-start | bytes 786440 | tf_op jit(solution)/shard_map/ppermute | solution.py:26
  69.2 13.2 %collective-permute-start.19 = (bf16[16,8192]{1,0:T(8,128)(2,1)S(1)}, bf16[16,8192]{1,0:T(8,128)(2,1)S(1)}, u32[]{:S(2)}, u32[]{:S(2)}) collective-permute-start(bf16[16,8192]{1,0:T(8,128)(2,1)S(1)} %get-tuple-element.116), channel_id=1, source_target_pairs={{0,6},{1,7},{2,0},{3,1},{4,2},{5,3},{6,4},{7,5},{8,14},{9,15},{10,... | collective-permute-start | bytes 786440 | tf_op jit(solution)/shard_map/ppermute | solution.py:26
  76.1 22.1 %collective-permute-start.23 = (bf16[256,1024]{1,0:T(8,128)(2,1)S(1)}, bf16[256,1024]{1,0:T(8,128)(2,1)S(1)}, u32[]{:S(2)}, u32[]{:S(2)}) collective-permute-start(bf16[256,1024]{1,0:T(8,128)(2,1)S(1)} %get-tuple-element.101), channel_id=1, source_target_pairs={{0,8},{8,16},{16,24},{24,32},{32,40},{40,48},{48,56},{56,0},{64,72... | collective-permute-start | bytes 1572872 | tf_op jit(solution)/shard_map/ppermute | solution.py:38
  78.1 20.1 %collective-permute-start.24 = (bf16[256,1024]{1,0:T(8,128)(2,1)S(1)}, bf16[256,1024]{1,0:T(8,128)(2,1)S(1)}, u32[]{:S(2)}, u32[]{:S(2)}) collective-permute-start(bf16[256,1024]{1,0:T(8,128)(2,1)S(1)} %get-tuple-element.102), channel_id=1, source_target_pairs={{0,56},{8,0},{16,8},{24,16},{32,24},{40,32},{48,40},{56,48},{64,12... | collective-permute-start | bytes 1572872 | tf_op jit(solution)/shard_map/ppermute | solution.py:38
  82.4 15.8 %collective-permute-start.21 = (bf16[64,1024]{1,0:T(8,128)(2,1)S(1)}, bf16[64,1024]{1,0:T(8,128)(2,1)S(1)}, u32[]{:S(2)}, u32[]{:S(2)}) collective-permute-start(bf16[64,1024]{1,0:T(8,128)(2,1)S(1)} %get-tuple-element.127), channel_id=1, source_target_pairs={{0,16},{8,24},{16,32},{24,40},{32,48},{40,56},{48,0},{56,8},{64,80... | collective-permute-start | bytes 393224 | tf_op jit(solution)/shard_map/ppermute | solution.py:38
  82.5 15.8 %collective-permute-start.22 = (bf16[64,1024]{1,0:T(8,128)(2,1)S(1)}, bf16[64,1024]{1,0:T(8,128)(2,1)S(1)}, u32[]{:S(2)}, u32[]{:S(2)}) collective-permute-start(bf16[64,1024]{1,0:T(8,128)(2,1)S(1)} %get-tuple-element.126), channel_id=1, source_target_pairs={{0,48},{8,56},{16,0},{24,8},{32,16},{40,24},{48,32},{56,40},{64,11... | collective-permute-start | bytes 393224 | tf_op jit(solution)/shard_map/ppermute | solution.py:38
  86.7 28.4 %collective-permute-start.20 = (bf16[32,8192]{1,0:T(8,128)(2,1)S(1)}, bf16[32,8192]{1,0:T(8,128)(2,1)S(1)}, u32[]{:S(2)}, u32[]{:S(2)}) collective-permute-start(bf16[32,8192]{1,0:T(8,128)(2,1)S(1)} %get-tuple-element.98), channel_id=1, source_target_pairs={{0,2},{1,3},{2,4},{3,5},{4,6},{5,7},{6,0},{7,1},{8,10},{9,11},{10,... | collective-permute-start | bytes 1572872 | tf_op jit(solution)/shard_map/ppermute | solution.py:26
  98.2 16.9 %collective-permute-start.25 = (bf16[32,8192]{1,0:T(8,128)(2,1)S(1)}, bf16[32,8192]{1,0:T(8,128)(2,1)S(1)}, u32[]{:S(2)}, u32[]{:S(2)}) collective-permute-start(bf16[32,8192]{1,0:T(8,128)(2,1)S(1)} %get-tuple-element.105), channel_id=1, source_target_pairs={{0,6},{1,7},{2,0},{3,1},{4,2},{5,3},{6,4},{7,5},{8,14},{9,15},{10,... | collective-permute-start | bytes 1572872 | tf_op jit(solution)/shard_map/ppermute | solution.py:26
  99.4 11.9 %collective-permute-start.26 = (bf16[128,1024]{1,0:T(8,128)(2,1)S(1)}, bf16[128,1024]{1,0:T(8,128)(2,1)S(1)}, u32[]{:S(2)}, u32[]{:S(2)}) collective-permute-start(bf16[128,1024]{1,0:T(8,128)(2,1)S(1)} %get-tuple-element.112), channel_id=1, source_target_pairs={{0,16},{8,24},{16,32},{24,40},{32,48},{40,56},{48,0},{56,8},{64,80... | collective-permute-start | bytes 786440 | tf_op jit(solution)/shard_map/ppermute | solution.py:38
  103.9 9.6 %collective-permute-start.27 = (bf16[128,1024]{1,0:T(8,128)(2,1)S(1)}, bf16[128,1024]{1,0:T(8,128)(2,1)S(1)}, u32[]{:S(2)}, u32[]{:S(2)}) collective-permute-start(bf16[128,1024]{1,0:T(8,128)(2,1)S(1)} %get-tuple-element.113), channel_id=1, source_target_pairs={{0,48},{8,56},{16,0},{24,8},{32,16},{40,24},{48,32},{56,40},{64,11... | collective-permute-start | bytes 786440 | tf_op jit(solution)/shard_map/ppermute | solution.py:38
  (11 other events, 96.6 us)
